TPU v7x, 256 devices: a whole 4x4x8 slice. The times are simulated.
256 devices in a mesh: pb: 4 (over y), neg: 64 (over z, x, core).
Axes of the slice: x: 4, y: 4, z: 8, core: 2. Of those that a mesh axis runs over, the one named last changes fastest.
Arguments:
- hidden: bfloat16 [4, 256, 128, 1024], P('pb', 'neg'), may hold values from -6 to 6
- lengths: int32 [4, 256], P('pb', 'neg'), may hold values from 32 to 128
- teacher: float32 [4, 256], P('pb', 'neg'), may hold values from -8 to 8
- norm_gain: float32 [1024], replicated, may hold values from 0.1 to 1.9
- final_gain: float32 [1024], replicated, may hold values from 0.1 to 1.9
- score_vector: float32 [1024], replicated, may hold values from -0.1875 to 0.1875
- query_weight: bfloat16 [1024, 1024], P(('pb', 'neg')), may hold values from -0.1875 to 0.1875
- key_matrix: bfloat16 [1024, 512], P(('pb', 'neg')), may hold values from -0.1875 to 0.1875
- value_matrix: bfloat16 [1024, 512], P(('pb', 'neg')), may hold values from -0.1875 to 0.1875
- out_weight: bfloat16 [1024, 1024], P(None, ('pb', 'neg')), may hold values from -0.1875 to 0.1875
Outputs:
- scores: float32 [4, 256], P('pb', 'neg')
- loss: float32 [], replicated
- grad_hidden: bfloat16 [4, 256, 128, 1024], P('pb', 'neg')
- grad_query: float32 [1024, 1024], P(('pb', 'neg'))
- grad_key: float32 [1024, 512], P(('pb', 'neg'))
- grad_value: float32 [1024, 512], P(('pb', 'neg'))
- grad_out: float32 [1024, 1024], P(None, ('pb', 'neg'))
Inputs may be any that keep to these rules, and one draw needn't show every extreme that they name: `lengths`: the number of real tokens of the pair; its other positions out of 128 are padding.
All inputs are finite; a program needn't handle non-finite values.
Results may differ from a plain program's by a relative error of at most 0.013.
Values may be sent and summed in bfloat16 or wider, within the bound.
No kernel may reach another device: no remote copies, remote signals or barrier semaphores. Data moves between devices by JAX's collectives and lax.ppermute only.
A program may use at most 64 MiB of HBM per device.

v0:
```python
import jax
import jax.numpy as jnp
from jax import lax
from jax.sharding import Mesh
from jax.sharding import PartitionSpec as P

HEAD_WIDTH = 128
PB_NEG = ("pb", "neg_0", "neg_1", "neg_2")
NEG = ("neg_0", "neg_1", "neg_2")


EPSILON = 1e-06
ROPE_BASE = 1000000.0
TEACHER_TEMP = 2.0
GRAD_SCALE = 512.0


def gather_turned(arrays, axis, dims):
    turned = [jnp.moveaxis(a, dim, 0) for a, dim in zip(arrays, dims)]
    both = jnp.concatenate([t.reshape(len(t), -1) for t in turned], axis=1)
    out, at, outs = (lax.all_gather(both, axis, axis=0, tiled=True), 0, [])
    for t, dim in zip(turned, dims):
        slab = out[:, at : at + t[0].size].reshape(-1, *t.shape[1:])
        outs.append(jnp.moveaxis(slab, 0, dim))
        at += t[0].size
    return tuple(outs)


def from_everyone(shard, axis):
    count = lax.axis_size(axis)
    return lax.all_to_all(
        jnp.broadcast_to(shard[None], (count, *shard.shape)), axis, 0, 0, tiled=True
    )


def taken_together(shard, axis):
    return from_everyone(shard, axis).sum(axis=0)


def in_one(arrays, axis):
    flat, at, outs = (jnp.concatenate([a.reshape(-1) for a in arrays]), 0, [])
    subtotal = taken_together(flat, axis)
    for a in arrays:
        outs.append(subtotal[at : at + a.size].reshape(a.shape))
        at += a.size
    return tuple(outs)


def one_axis_at_a_time(shard, axes):
    for axis in axes:
        shard = lax.psum(shard, axis)
    return shard


def sent_together(arrays, axis, dim, along):
    ends, at = ([], 0)
    for a in arrays[:-1]:
        at += a.shape[along]
        ends.append(at)
    both = jnp.concatenate(arrays, axis=along)
    return tuple(
        jnp.split(lax.psum_scatter(both, axis, scatter_dimension=dim, tiled=True), ends, axis=along)
    )


def cut_along(shard, dim, count):
    before, after = (shard.shape[:dim], shard.shape[dim + 1 :])
    return jnp.moveaxis(shard.reshape(*before, count, -1, *after), dim, 0)


def sum_packed(arrays, axis, dims):
    count = lax.axis_size(axis)
    tiles = [cut_along(a, dim, count) for a, dim in zip(arrays, dims)]
    lines = jnp.concatenate([b.reshape(count, -1) for b in tiles], axis=1)
    span = max(16, -(-lines.shape[1] // 1024) * 8)
    lines = jnp.pad(lines, ((0, 0), (0, span * 128 - lines.shape[1]))).reshape(-1, 128)
    flat, at, outs = (lax.psum_scatter(lines, axis, tiled=True).reshape(-1), 0, [])
    for b in tiles:
        part = b[0]
        outs.append(flat[at : at + part.size].reshape(part.shape))
        at += part.size
    return tuple(outs)


def rope_tables(seq_len, head_size):
    half = head_size // 2
    freqs = ROPE_BASE ** (-(jnp.arange(half, dtype=jnp.float32) * 2.0) / head_size)
    angles = jnp.arange(seq_len, dtype=jnp.float32)[:, None] * freqs[None, :]
    angles = jnp.concatenate([angles, angles], axis=1)
    return (jnp.cos(angles), jnp.sin(angles))


def rotate_half(vector):
    half = vector.shape[-1] // 2
    return jnp.concatenate([-vector[..., half:], vector[..., :half]], axis=-1)


def unrotate_half(vector):
    half = vector.shape[-1] // 2
    return jnp.concatenate([vector[..., half:], -vector[..., :half]], axis=-1)


def forward_pairs(
    tokens_in,
    lengths_here,
    norm_gain,
    final_gain,
    score_vector,
    query_weight,
    key_matrix,
    value_matrix,
    out_weight,
):
    pair_count, seq_len, model_width = tokens_in.shape
    head_count = query_weight.shape[1] // HEAD_WIDTH
    group_count = key_matrix.shape[1] // HEAD_WIDTH
    group_size = head_count // group_count
    inputs_wide = tokens_in.astype(jnp.float32)
    inv_rms = lax.rsqrt(jnp.mean(inputs_wide * inputs_wide, axis=-1, keepdims=True) + EPSILON)
    normed = (inputs_wide * inv_rms * norm_gain).astype(jnp.bfloat16)
    flat_rows = normed.reshape(pair_count * seq_len, model_width)
    key_proj = jnp.dot(flat_rows, key_matrix, preferred_element_type=jnp.float32).reshape(
        pair_count, seq_len, group_count, HEAD_WIDTH
    )
    value_proj = jnp.dot(flat_rows, value_matrix, preferred_element_type=jnp.float32).reshape(
        pair_count, seq_len, group_count, HEAD_WIDTH
    )
    positions = jnp.arange(seq_len, dtype=jnp.int32)
    last_index = lengths_here - 1
    onehot = (positions[None, :] == last_index[:, None]).astype(jnp.float32)
    normed_last = jnp.take_along_axis(normed, last_index[:, None, None], axis=1)[:, 0]
    query_proj = jnp.dot(normed_last, query_weight, preferred_element_type=jnp.float32).reshape(
        pair_count, head_count, HEAD_WIDTH
    )
    query_scale = lax.rsqrt(jnp.mean(query_proj * query_proj, axis=-1, keepdims=True) + EPSILON)
    query_unit = query_proj * query_scale
    key_scale = lax.rsqrt(jnp.mean(key_proj * key_proj, axis=-1, keepdims=True) + EPSILON)
    key_unit = key_proj * key_scale
    cos_table, sin_table = rope_tables(seq_len, HEAD_WIDTH)
    cos_query = jnp.dot(onehot, cos_table, precision=lax.Precision.HIGHEST)
    sin_query = jnp.dot(onehot, sin_table, precision=lax.Precision.HIGHEST)
    query_rot = (
        query_unit * cos_query[:, None, :] + rotate_half(query_unit) * sin_query[:, None, :]
    ).astype(jnp.bfloat16)
    key_rot = (
        key_unit * cos_table[None, :, None, :] + rotate_half(key_unit) * sin_table[None, :, None, :]
    ).astype(jnp.bfloat16)
    value_cast = value_proj.astype(jnp.bfloat16)
    grouped = query_rot.reshape(pair_count, group_count, group_size, HEAD_WIDTH)
    logits = jnp.einsum(
        "pkgd,pskd->pkgs", grouped, key_rot, preferred_element_type=jnp.float32
    ) * HEAD_WIDTH ** (-0.5)
    visible = (positions[None, :] <= last_index[:, None])[:, None, None, :]
    expos = jnp.where(visible, jnp.exp(logits), 0.0)
    attention_weights = expos / jnp.sum(expos, axis=-1, keepdims=True)
    probs_cast = attention_weights.astype(jnp.bfloat16)
    context = jnp.einsum(
        "pkgs,pskd->pkgd", probs_cast, value_cast, preferred_element_type=jnp.float32
    )
    context = context.astype(jnp.bfloat16).reshape(pair_count, head_count * HEAD_WIDTH)
    attended = jnp.dot(context, out_weight, preferred_element_type=jnp.float32)
    residual = jnp.take_along_axis(inputs_wide, last_index[:, None, None], axis=1)[:, 0] + attended
    out_scale = lax.rsqrt(jnp.mean(residual * residual, axis=-1, keepdims=True) + EPSILON)
    out_unit = residual * out_scale
    scores_here = jnp.sum(out_unit * final_gain * score_vector, axis=-1)
    stored = (
        tokens_in,
        onehot,
        inv_rms,
        normed,
        normed_last,
        query_unit,
        query_scale,
        key_unit,
        key_scale,
        cos_query,
        sin_query,
        cos_table,
        sin_table,
        query_rot,
        key_rot,
        value_cast,
        attention_weights,
        probs_cast,
        context,
        out_unit,
        out_scale,
    )
    return (scores_here, stored)


def backward_pairs(
    stored,
    grad_score,
    norm_gain,
    final_gain,
    score_vector,
    query_weight,
    key_matrix,
    value_matrix,
    out_weight,
):
    (
        tokens_in,
        onehot,
        inv_rms,
        normed,
        normed_last,
        query_unit,
        query_scale,
        key_unit,
        key_scale,
        cos_query,
        sin_query,
        cos_table,
        sin_table,
        query_rot,
        key_rot,
        value_cast,
        attention_weights,
        probs_cast,
        context,
        out_unit,
        out_scale,
    ) = stored
    pair_count, seq_len, model_width = tokens_in.shape
    head_count = query_weight.shape[1] // HEAD_WIDTH
    group_count = key_matrix.shape[1] // HEAD_WIDTH
    group_size = head_count // group_count
    grad_unit = grad_score[:, None] * score_vector * final_gain
    grad_resid = out_scale * (
        grad_unit - out_unit * jnp.mean(grad_unit * out_unit, axis=-1, keepdims=True)
    )
    grad_resid_cast = grad_resid.astype(jnp.bfloat16)
    grad_out = jnp.dot(context.T, grad_resid_cast, preferred_element_type=jnp.float32)
    grad_context = jnp.dot(
        grad_resid_cast, out_weight.T, preferred_element_type=jnp.float32
    ).astype(jnp.bfloat16)
    grad_context = grad_context.reshape(pair_count, group_count, group_size, HEAD_WIDTH)
    grad_probs = jnp.einsum(
        "pkgd,pskd->pkgs", grad_context, value_cast, preferred_element_type=jnp.float32
    )
    grad_vals = jnp.einsum(
        "pkgs,pkgd->pskd", probs_cast, grad_context, preferred_element_type=jnp.float32
    )
    spread = jnp.sum(attention_weights * grad_probs, axis=-1, keepdims=True)
    logit_gradient = (attention_weights * (grad_probs - spread)).astype(jnp.bfloat16)
    grouped = query_rot.reshape(pair_count, group_count, group_size, HEAD_WIDTH)
    rotated_query_gradient = jnp.einsum(
        "pkgs,pskd->pkgd", logit_gradient, key_rot, preferred_element_type=jnp.float32
    ) * HEAD_WIDTH ** (-0.5)
    rotated_query_gradient = rotated_query_gradient.reshape(pair_count, head_count, HEAD_WIDTH)
    grad_krot = jnp.einsum(
        "pkgs,pkgd->pskd", logit_gradient, grouped, preferred_element_type=jnp.float32
    ) * HEAD_WIDTH ** (-0.5)
    grad_qunit = rotated_query_gradient * cos_query[:, None, :] + unrotate_half(
        rotated_query_gradient * sin_query[:, None, :]
    )
    grad_kunit = grad_krot * cos_table[None, :, None, :] + unrotate_half(
        grad_krot * sin_table[None, :, None, :]
    )
    grad_qproj = query_scale * (
        grad_qunit - query_unit * jnp.mean(grad_qunit * query_unit, axis=-1, keepdims=True)
    )
    grad_kproj = key_scale * (
        grad_kunit - key_unit * jnp.mean(grad_kunit * key_unit, axis=-1, keepdims=True)
    )
    grad_q_cast = grad_qproj.reshape(pair_count, head_count * HEAD_WIDTH).astype(jnp.bfloat16)
    grad_k_cast = grad_kproj.reshape(pair_count * seq_len, group_count * HEAD_WIDTH).astype(
        jnp.bfloat16
    )
    grad_v_cast = grad_vals.reshape(pair_count * seq_len, group_count * HEAD_WIDTH).astype(
        jnp.bfloat16
    )
    flat_rows = normed.reshape(pair_count * seq_len, model_width)
    grad_query = jnp.dot(normed_last.T, grad_q_cast, preferred_element_type=jnp.float32)
    grad_key = jnp.dot(flat_rows.T, grad_k_cast, preferred_element_type=jnp.float32)
    grad_value = jnp.dot(flat_rows.T, grad_v_cast, preferred_element_type=jnp.float32)
    grad_normed = jnp.dot(grad_k_cast, key_matrix.T, preferred_element_type=jnp.float32)
    grad_normed = grad_normed + jnp.dot(
        grad_v_cast, value_matrix.T, preferred_element_type=jnp.float32
    )
    grad_normed = grad_normed.reshape(pair_count, seq_len, model_width)
    grad_last = jnp.dot(grad_q_cast, query_weight.T, preferred_element_type=jnp.float32)
    grad_normed = grad_normed + onehot[:, :, None] * grad_last[:, None, :]
    inputs_wide = tokens_in.astype(jnp.float32)
    grad_scaled = grad_normed * norm_gain
    grad_input = inv_rms * grad_scaled - inputs_wide * inv_rms * inv_rms * inv_rms * jnp.mean(
        grad_scaled * inputs_wide, axis=-1, keepdims=True
    )
    grad_input = grad_input + onehot[:, :, None] * grad_resid[:, None, :]
    return (grad_input.astype(jnp.bfloat16), (grad_query, grad_key, grad_value, grad_out))


def shards(
    hidden,
    lengths,
    teacher,
    norm_gain,
    final_gain,
    score_vector,
    query_weight,
    key_matrix,
    value_matrix,
    out_weight,
):
    tokens_in = hidden[0]
    lengths_here = lengths[0]
    gathered = gather_turned(
        (query_weight, key_matrix, value_matrix, out_weight), PB_NEG, (0, 0, 0, 1)
    )
    scores_here, stored = forward_pairs(
        tokens_in,
        lengths_here,
        norm_gain,
        final_gain,
        score_vector,
        gathered[0],
        gathered[1],
        gathered[2],
        gathered[3],
    )
    scaled = teacher[0] / TEACHER_TEMP
    expo_s = jnp.exp(scores_here)
    expo_t = jnp.exp(scaled)
    total_s, total_t = in_one((jnp.sum(expo_s), jnp.sum(expo_t)), NEG)
    prob_s = expo_s / total_s
    prob_t = expo_t / total_t
    local_terms = jnp.sum(prob_t * (scaled - jnp.log(total_t) - (scores_here - jnp.log(total_s))))
    loss_value = one_axis_at_a_time(local_terms, PB_NEG)
    grad_score = GRAD_SCALE * (prob_s - prob_t)
    weights_back = gather_turned(
        (query_weight, key_matrix, value_matrix, out_weight), PB_NEG, (0, 0, 0, 1)
    )
    grad_input, grads = backward_pairs(
        stored,
        grad_score,
        norm_gain,
        final_gain,
        score_vector,
        weights_back[0],
        weights_back[1],
        weights_back[2],
        weights_back[3],
    )
    by_query = (
        *tuple(
            (
                part.astype(jnp.float32)
                for part in sent_together(
                    (
                        grads[0].astype(jnp.bfloat16),
                        grads[1].astype(jnp.bfloat16),
                        grads[2].astype(jnp.bfloat16),
                    ),
                    "pb",
                    0,
                    1,
                )
            )
        ),
        lax.psum_scatter(
            grads[3].astype(jnp.bfloat16), "pb", scatter_dimension=1, tiled=True
        ).astype(jnp.float32),
    )
    reduced = sum_packed((by_query[0], by_query[1], by_query[2], by_query[3]), NEG, (0, 0, 0, 1))
    return (
        scores_here[None],
        loss_value,
        grad_input[None],
        reduced[0],
        reduced[1],
        reduced[2],
        reduced[3],
    )


def solution(mesh):
    torus = Mesh(mesh.devices.reshape(mesh.shape["pb"], 8, 4, 2), ("pb", "neg_0", "neg_1", "neg_2"))
    placed = (
        P("pb", NEG, None, None),
        P("pb", NEG),
        P("pb", NEG),
        P(),
        P(),
        P(),
        P(PB_NEG, None),
        P(PB_NEG, None),
        P(PB_NEG, None),
        P(None, PB_NEG),
    )
    return jax.shard_map(
        shards,
        mesh=torus,
        in_specs=placed,
        out_specs=(
            P("pb", NEG),
            P(),
            P("pb", NEG, None, None),
            P(PB_NEG, None),
            P(PB_NEG, None),
            P(PB_NEG, None),
            P(None, PB_NEG),
        ),
        check_vma=False,
    )
```

profile of v0, /device:TPU:1, one launch (start us, length us, event | category | flops | bytes accessed | tf_op | source)
XLA Modules:
  0.0 427.7 jit_solution(12811311809700793395)
XLA Ops:
  17.2 115.5 %all-gather.3.cloned.1.call-done = bf16[256,4,3072]{2,1,0:T(4,128)(2,1)} async-done(((bf16[1,4,3072]{2,1,0:T(4,128)(2,1)}), bf16[256,4,3072]{2,1,0:T(4,128)(2,1)}) %all-gather.3.cloned.1.call-update) | async-done | bytes 6291472 | tf_op jit(solution)/shard_map/all_gather | solution.py:21
  132.7 10.6 %reshape.509 = bf16[1024,3072]{1,0:T(8,128)(2,1)} reshape(bf16[256,4,3072]{2,1,0:T(4,128)(2,1)} %all-gather.3.cloned.1.call-done) | data formatting | bytes 12582912
  143.3 3.2 fusion.67
  146.6 2.6 copy.98
  149.2 2.5 multiply_reduce_fusion.8
  156.3 2.3 copy.100
  158.6 3.2 convolution_convert_fusion.5
  163.7 2.4 multiply_reduce_fusion.7
  168.3 17.0 %all_to_all.6 = f32[64,1,2]{2,1,0:T(1,128)S(1)} all-to-all(f32[64,1,2]{2,1,0:T(1,128)S(1)} %broadcast_in_dim.39), channel_id=1, replica_groups=mesh['pb'=4,'neg_0'=8,'neg_1'=4,'neg_2'=2] {'neg_0','neg_1','neg_2'}, dimensions={0} | all-to-all | bytes 1024 | tf_op jit(solution)/shard_map/all_to_all | solution.py:31
  187.6 2.0 fusion.13
  189.6 2.1 convolution_convert_fusion
  200.7 2.4 pad_maximum_fusion
  203.1 14.9 %reduce-scatter.6.cloned.1.call-done = bf16[1024,256]{1,0:T(8,128)(2,1)} async-done(((bf16[1024,1024]{1,0:T(8,128)(2,1)}), bf16[1024,256]{1,0:T(8,128)(2,1)}) %reduce-scatter.6.cloned.1.call-update) | async-done | bytes 524304 | tf_op jit(solution)/shard_map/reduce_scatter | solution.py:362
  220.7 49.2 %reduce-scatter.4.cloned.1.call-done = bf16[256,2048]{0,1:T(8,128)(2,1)} async-done(((bf16[1024,2048]{0,1:T(8,128)(2,1)}), bf16[256,2048]{0,1:T(8,128)(2,1)}) %reduce-scatter.4.cloned.1.call-update) | async-done | bytes 1048592 | tf_op jit(solution)/shard_map/reduce_scatter | solution.py:62
  275.6 4.3 %reshape.489 = f32[6144,128]{1,0:T(8,128)} reshape(f32[64,12288]{1,0:T(8,128)} %maximum_convert_fusion) | data formatting | bytes 6291456 | tf_op jit(solution)/shard_map/reshape | solution.py:76
  282.0 7.1 %psum.28 = f32[]{:T(128)} all-reduce(f32[]{:T(128)} %fusion.54), channel_id=1, replica_groups=mesh['pb'=4,'neg_0'=8,'neg_1'=4,'neg_2'=2] {'pb'}, use_global_device_ids=true, to_apply=%region_10.11 | all-reduce | flops 1 | bytes 8 | tf_op jit(solution)/shard_map/psum | solution.py:51
  289.1 14.3 %psum.29 = f32[]{:T(128)} all-reduce(f32[]{:T(128)} %psum.28), channel_id=1, replica_groups=mesh['pb'=4,'neg_0'=8,'neg_1'=4,'neg_2'=2] {'neg_0'}, use_global_device_ids=true, to_apply=%region_11.12 | all-reduce | flops 1 | bytes 8 | tf_op jit(solution)/shard_map/psum | solution.py:51
  303.4 9.0 %psum.30 = f32[]{:T(128)} all-reduce(f32[]{:T(128)} %psum.29), channel_id=1, replica_groups=mesh['pb'=4,'neg_0'=8,'neg_1'=4,'neg_2'=2] {'neg_1'}, use_global_device_ids=true, to_apply=%region_12.13 | all-reduce | flops 1 | bytes 8 | tf_op jit(solution)/shard_map/psum | solution.py:51
  312.4 11.2 %psum.31 = f32[]{:T(128)} all-reduce(f32[]{:T(128)} %psum.30), channel_id=1, replica_groups=mesh['pb'=4,'neg_0'=8,'neg_1'=4,'neg_2'=2] {'neg_2'}, use_global_device_ids=true, to_apply=%region_13.14 | all-reduce | flops 1 | bytes 8 | tf_op jit(solution)/shard_map/psum | solution.py:51
  323.6 2.3 fusion.65
  325.9 2.1 fusion.24
  327.9 2.3 fusion
  330.2 2.5 add_convert_fusion
  332.7 83.9 %reduce-scatter.8.cloned.1.call-done = f32[96,128]{1,0:T(8,128)} async-done(((f32[6144,128]{1,0:T(8,128)}), f32[96,128]{1,0:T(8,128)}) %reduce-scatter.8.cloned.1.call-update) | async-done | bytes 49168 | tf_op jit(solution)/shard_map/reduce_scatter | solution.py:77
  (131 shorter events, 43.5 us)
Async XLA Ops:
  7.2 6.0 %copy-start = (bf16[1,4,128,1024]{3,2,1,0:T(8,128)(2,1)S(1)}, bf16[1,4,128,1024]{3,2,1,0:T(8,128)(2,1)}, u32[]{:S(2)}) copy-start(bf16[1,4,128,1024]{3,2,1,0:T(8,128)(2,1)} %param.10) | copy-start | bytes 3145732
  7.2 125.5 %all-gather.3.cloned.1.call-start = ((), (), s32[]{:S(2)}) async-start(), calls=%async_computation.7 | async-start | bytes 6316032 | tf_op jit(solution)/shard_map/all_gather | solution.py:21
  8.7 209.3 %reduce-scatter.6.cloned.1.call-start = ((), (), s32[]{:S(2)}) async-start(), calls=%async_computation.5 | async-start | bytes 2621440 | tf_op jit(solution)/shard_map/reduce_scatter | solution.py:362
  12.5 1.5 copy-start.13
  12.5 2.4 copy-start.14
  12.5 3.3 copy-start.9
  143.3 3.3 slice-start
  149.2 2.6 copy-start.1
  149.2 4.0 copy-start.6
  158.6 3.3 copy-start.2
  158.6 3.3 copy-start.3
  162.1 4.0 copy-start.10
  162.1 4.0 copy-start.11
  166.3 115.0 %copy-start.12 = (f32[4]{0:T(128)}, f32[4]{0:T(128)S(1)}, u32[]{:S(2)}) copy-start(f32[4]{0:T(128)S(1)} %multiply_reduce_fusion.6) | copy-start | bytes 52
  187.5 4.1 copy-start.8
  192.3 77.6 %reduce-scatter.4.cloned.1.call-start = ((), (), s32[]{:S(2)}) async-start(), calls=%async_computation.4 | async-start | bytes 5242880 | tf_op jit(solution)/shard_map/reduce_scatter | solution.py:62
  196.4 2.8 copy-start.4
  196.4 2.8 copy-start.7
  203.1 213.5 %reduce-scatter.8.cloned.1.call-start = ((), (), s32[]{:S(2)}) async-start(), calls=%async_computation.6 | async-start | bytes 3194880 | tf_op jit(solution)/shard_map/reduce_scatter | solution.py:77
  269.8 2.1 slice-start.1
  325.9 2.1 copy-start.5
Sparse Core Ops, SparseCore 0:
  12.4 120.2 all-gather.2
  192.4 25.6 reduce-scatter.5
  220.8 49.0 reduce-scatter.3
  280.1 136.4 reduce-scatter.7
where the time goes:
time: 433 us; the launch traced here: 428 us
  waiting for transfers between devices  264 us (61%)
  blocking collectives  58.6 us (14%)
  local copies, waits for them, and re-layouts  40 us (9%)
  matrix products  26.8 us (6%)
  other arithmetic  22.8 us (5%)
  between operations  15.6 us (4%)
    all_gather x1, waiting for transfers between devices, gather_turned(): out, at, outs = (lax.all_gather(both, axis, axis=0, tiled=True), 0, [])  116 us
    reduce_scatter x1, waiting for transfers between devices, sum_packed(): lax.psum_scatter(lines, axis, tiled=True).reshape(-1)  83.9 us
    reduce_scatter x1, waiting for transfers between devices, sent_together(): lax.psum_scatter(both, axis, scatter_dimension=dim, tiled=True)  49.2 us
    psum x4, blocking collectives, one_axis_at_a_time(): shard = lax.psum(shard, axis)  41.6 us
    unnamed x39, local copies, waits for them, and re-layouts  20.9 us
    all_to_all x1, blocking collectives, from_everyone(): lax.all_to_all(jnp.broadcast_to(shard[None], (count, *shard.shape)), axis...  17 us
    reduce_scatter x1, waiting for transfers between devices, shards(): lax.psum_scatter(grads[3].astype(jnp.bfloat16), 'pb', scatter_dimension=1...  14.9 us
  transfers between devices with their start and end apart: 4, of which 4 were waited for; matrix products, arithmetic and copies ran while one was open for 7% of the time, Pallas kernels for 0%

commit v1 on v0

v1 whole, which is shorter than its diff:
```python
import jax
import jax.numpy as jnp
import numpy as np
from jax import lax
from jax.experimental import pallas as pl
from jax.experimental.pallas import tpu as pltpu
from jax.sharding import Mesh
from jax.sharding import PartitionSpec as P

HW = 128
AXES = ("pb", "z", "x", "c")
NEG = ("z", "x", "c")
EPS = 1e-06
ROPE_BASE = 1000000.0
GRAD_SCALE = 512.0
PAIRS = 4
SEQ = 128
D = 1024
ROWS = PAIRS * SEQ
F32 = jnp.float32
BF16 = jnp.bfloat16
VM = pl.BlockSpec(memory_space=pltpu.VMEM)
SM = pl.BlockSpec(memory_space=pltpu.SMEM)
LAST = (((1,), (1,)), ((), ()))
FIRST = (((0,), (0,)), ((), ()))
SCALE = HW ** (-0.5)


def rope_consts():
    freqs = np.float32(ROPE_BASE) ** (-(np.arange(HW // 2, dtype=np.float32) * 2.0) / HW)
    angles = np.arange(SEQ, dtype=np.float32)[:, None] * freqs.astype(np.float32)[None, :]
    angles = np.concatenate([angles, angles], axis=1)
    sign = np.where(np.arange(HW) < HW // 2, -1.0, 1.0)
    return (
        np.cos(angles).astype(np.float32),
        (np.sin(angles) * sign[None, :]).astype(np.float32),
    )


def call(body, outs, in_specs, vmem=48, flops=0, nbytes=0):
    return pl.pallas_call(
        body,
        out_shape=[jax.ShapeDtypeStruct(s, d) for s, d in outs],
        in_specs=in_specs,
        out_specs=[VM] * len(outs),
        compiler_params=pltpu.CompilerParams(vmem_limit_bytes=vmem << 20),
        cost_estimate=pl.CostEstimate(flops=flops, bytes_accessed=nbytes, transcendentals=0),
    )


def dot(a, b, dims=(((1,), (0,)), ((), ()))):
    return lax.dot_general(a, b, dims, preferred_element_type=F32)


def half_turn(v):
    return pltpu.roll(v, HW // 2, 1)


def heads(v, n):
    return [v[:, i * HW : (i + 1) * HW] for i in range(n)]


def block_mask():
    row = lax.broadcasted_iota(jnp.int32, (8, 512), 0)
    lane = lax.broadcasted_iota(jnp.int32, (8, 512), 1)
    return (lane // HW) == (row // 2), (row % 2) == 0


def to_blocks(row, mask, even):
    h = heads(row, 8)
    e = jnp.broadcast_to(jnp.concatenate(h[0::2], axis=1), (8, 512))
    o = jnp.broadcast_to(jnp.concatenate(h[1::2], axis=1), (8, 512))
    return jnp.where(mask, jnp.where(even, e, o), 0.0)


def from_blocks(blocks, mask, even):
    e = jnp.sum(jnp.where(mask & even, blocks, 0.0), axis=0, keepdims=True)
    o = jnp.sum(jnp.where(mask & (~even), blocks, 0.0), axis=0, keepdims=True)
    parts = []
    for g in range(4):
        parts += [e[:, g * HW : (g + 1) * HW], o[:, g * HW : (g + 1) * HW]]
    return jnp.concatenate(parts, axis=1)


def prep_body(len_ref, h_ref, gain_ref, normed_ref, turned_ref, nlast_ref, xlast_ref):
    row = lax.broadcasted_iota(jnp.int32, (8, SEQ), 0)
    lane = lax.broadcasted_iota(jnp.int32, (8, SEQ), 1)
    nl = jnp.zeros((8, D), F32)
    xl = jnp.zeros((8, D), F32)
    for p in range(PAIRS):
        raw = h_ref[p * SEQ : (p + 1) * SEQ, :]
        x = raw.astype(F32)
        inv = lax.rsqrt(jnp.mean(x * x, axis=-1, keepdims=True) + EPS)
        n = (x * inv * gain_ref[...]).astype(BF16)
        normed_ref[p * SEQ : (p + 1) * SEQ, :] = n
        turned_ref[:, p * SEQ : (p + 1) * SEQ] = n.T
        e = len_ref[p] - 1
        hot = jnp.where((row == p) & (lane == e), 1.0, 0.0).astype(BF16)
        nl = nl + dot(hot, n)
        xl = xl + dot(hot, raw)
    nlast_ref[...] = nl.astype(BF16)
    xlast_ref[...] = xl


def attend_body(
    len_ref,
    normed_ref,
    nlast_ref,
    wa_ref,
    wb_ref,
    cos_ref,
    sin_ref,
    kproj_ref,
    krot_ref,
    vcast_ref,
    qproj_ref,
    qrot_ref,
    attn_ref,
    ctx_ref,
    qr_scr,
    ctx_scr,
):
    mask, even = block_mask()
    lane = lax.broadcasted_iota(jnp.int32, (8, SEQ), 1)
    for half, w_ref in enumerate((wa_ref, wb_ref)):
        kv = dot(normed_ref[...], w_ref[:, 0:512])
        kproj_ref[:, half * 256 : half * 256 + 256] = kv[:, 0:256]
        vcast_ref[:, half * 256 : half * 256 + 256] = kv[:, 256:512].astype(BF16)
        qproj_ref[:, half * 512 : half * 512 + 512] = dot(nlast_ref[...], w_ref[:, 512:1024])
    cos_q = jnp.concatenate(
        [cos_ref[pl.ds(len_ref[p] - 1, 1), :] for p in range(PAIRS)] * 2, axis=0
    )
    sin_q = jnp.concatenate(
        [sin_ref[pl.ds(len_ref[p] - 1, 1), :] for p in range(PAIRS)] * 2, axis=0
    )
    for h in range(8):
        q = qproj_ref[:, h * HW : (h + 1) * HW]
        u = q * lax.rsqrt(jnp.mean(q * q, axis=-1, keepdims=True) + EPS)
        r = u * cos_q + half_turn(u) * sin_q
        qr_scr[:, h * HW : (h + 1) * HW] = r
        qrot_ref[:, h * HW : (h + 1) * HW] = r.astype(BF16)
    ctx_scr[...] = jnp.zeros((8, D), F32)
    for p in range(PAIRS):
        rows = slice(p * SEQ, (p + 1) * SEQ)
        for g in range(4):
            k = kproj_ref[rows, g * HW : (g + 1) * HW]
            u = k * lax.rsqrt(jnp.mean(k * k, axis=-1, keepdims=True) + EPS)
            r = u * cos_ref[...] + half_turn(u) * sin_ref[...]
            krot_ref[rows, g * HW : (g + 1) * HW] = r.astype(BF16)
        qb = to_blocks(qr_scr[p : p + 1, :], mask, even).astype(BF16)
        logits = dot(qb, krot_ref[rows, :], LAST) * SCALE
        ex = jnp.where(lane <= len_ref[p] - 1, jnp.exp(logits), 0.0)
        w = ex / jnp.sum(ex, axis=-1, keepdims=True)
        attn_ref[p * 8 : (p + 1) * 8, :] = w
        c = dot(w.astype(BF16), vcast_ref[rows, :])
        ctx_scr[p : p + 1, :] = from_blocks(c, mask, even)
    ctx_ref[...] = ctx_scr[...].astype(BF16)


def score_body(
    teach_ref, ctx_ref, xlast_ref, oa_ref, ob_ref, fg_ref, sv_ref, unit_ref, oscale_ref, score_ref, tot_ref
):
    res = xlast_ref[...] + (
        dot(ctx_ref[:, 0:512], oa_ref[...], LAST) + dot(ctx_ref[:, 512:1024], ob_ref[...], LAST)
    )
    sc = lax.rsqrt(jnp.mean(res * res, axis=-1, keepdims=True) + EPS)
    unit = res * sc
    unit_ref[...] = unit
    oscale_ref[...] = jnp.broadcast_to(sc, (8, HW))
    s = jnp.sum(unit * fg_ref[...] * sv_ref[...], axis=-1, keepdims=True)
    s = jnp.broadcast_to(s, (8, HW))
    score_ref[...] = s
    row = lax.broadcasted_iota(jnp.int32, (8, HW), 0)
    lane = lax.broadcasted_iota(jnp.int32, (8, HW), 1)
    scaled = teach_ref[...] / 2.0
    es = jnp.exp(s)
    et = jnp.exp(scaled)
    v = jnp.where(lane == 0, es, jnp.where(lane == 1, et, et * (scaled - s)))
    v = jnp.where((row < PAIRS) & (lane < 3), v, 0.0)
    tot_ref[...] = jnp.broadcast_to(jnp.sum(v, axis=0, keepdims=True), (8, HW))


def unit_back_body(
    len_ref,
    krot_ref,
    vcast_ref,
    kproj_ref,
    qproj_ref,
    qrot_ref,
    attn_ref,
    unit_ref,
    oscale_ref,
    oa_ref,
    ob_ref,
    fg_ref,
    sv_ref,
    cos_ref,
    sin_ref,
    gkva_ref,
    gkvb_ref,
    gq_ref,
    gr_ref,
    gc_scr,
    gq_scr,
    qr_scr,
):
    mask, even = block_mask()
    unit = unit_ref[...]
    gu = sv_ref[...] * fg_ref[...]
    gr = oscale_ref[:, 0:1] * (gu - unit * jnp.mean(gu * unit, axis=-1, keepdims=True))
    gr_ref[...] = gr
    grb = gr.astype(BF16)
    gc_scr[:, 0:512] = dot(grb, oa_ref[...])
    gc_scr[:, 512:1024] = dot(grb, ob_ref[...])
    qr_scr[...] = qrot_ref[...].astype(F32)
    gq_scr[...] = jnp.zeros((8, D), F32)
    for p in range(PAIRS):
        rows = slice(p * SEQ, (p + 1) * SEQ)
        gb = to_blocks(gc_scr[p : p + 1, :], mask, even).astype(BF16)
        qb = to_blocks(qr_scr[p : p + 1, :], mask, even).astype(BF16)
        w = attn_ref[p * 8 : (p + 1) * 8, :]
        gp = dot(gb, vcast_ref[rows, :], LAST)
        gv = dot(w.astype(BF16), gb, FIRST)
        gkva_ref[rows, 256:512] = gv[:, 0:256]
        gkvb_ref[rows, 256:512] = gv[:, 256:512]
        spread = jnp.sum(w * gp, axis=-1, keepdims=True)
        dl = (w * (gp - spread)).astype(BF16)
        gq_scr[p : p + 1, :] = from_blocks(dot(dl, krot_ref[rows, :]) * SCALE, mask, even)
        gk = dot(dl, qb, FIRST) * SCALE
        for g in range(4):
            k = kproj_ref[rows, g * HW : (g + 1) * HW]
            sc = lax.rsqrt(jnp.mean(k * k, axis=-1, keepdims=True) + EPS)
            u = k * sc
            r = gk[:, g * HW : (g + 1) * HW]
            t = r * cos_ref[...] + half_turn(r * sin_ref[...])
            out = sc * (t - u * jnp.mean(t * u, axis=-1, keepdims=True))
            ref = gkva_ref if g < 2 else gkvb_ref
            ref[rows, (g % 2) * HW : (g % 2 + 1) * HW] = out
    cos_q = jnp.concatenate(
        [cos_ref[pl.ds(len_ref[p] - 1, 1), :] for p in range(PAIRS)] * 2, axis=0
    )
    sin_q = jnp.concatenate(
        [sin_ref[pl.ds(len_ref[p] - 1, 1), :] for p in range(PAIRS)] * 2, axis=0
    )
    for h in range(8):
        q = qproj_ref[:, h * HW : (h + 1) * HW]
        sc = lax.rsqrt(jnp.mean(q * q, axis=-1, keepdims=True) + EPS)
        u = q * sc
        r = gq_scr[:, h * HW : (h + 1) * HW]
        t = r * cos_q + half_turn(r * sin_q)
        gq_ref[:, h * HW : (h + 1) * HW] = sc * (
            t - u * jnp.mean(t * u, axis=-1, keepdims=True)
        )


def weight_body(
    pb_ref,
    tot_ref,
    score_ref,
    teach_ref,
    gkva_ref,
    gkvb_ref,
    gq_ref,
    gr_ref,
    turned_ref,
    nlast_ref,
    ctx_ref,
    loss_ref,
    grad_a_ref,
    grad_b_ref,
    skva_ref,
    skvb_ref,
    sq_ref,
    sr_ref,
):
    pb = pb_ref[0]
    lane = lax.broadcasted_iota(jnp.int32, (1, HW), 1)

    def pick(v, i):
        return jnp.sum(jnp.where(lane == i, v, 0.0), axis=-1, keepdims=True)

    loss = jnp.zeros((1, 1), F32)
    mine = jnp.zeros((1, HW), F32)
    for q in range(4):
        t = jnp.sum(tot_ref[q * 64 : (q + 1) * 64, :], axis=0, keepdims=True)
        ts, tt, cr = pick(t, 0), pick(t, 1), pick(t, 2)
        loss = loss + (cr / tt - jnp.log(tt) + jnp.log(ts))
        mine = mine + jnp.where(pb == q, t, 0.0)
    loss_ref[...] = jnp.broadcast_to(loss, (8, HW))
    ts, tt = pick(mine, 0), pick(mine, 1)
    row = lax.broadcasted_iota(jnp.int32, (8, HW), 0)
    g = GRAD_SCALE * (jnp.exp(score_ref[...]) / ts - jnp.exp(teach_ref[...] / 2.0) / tt)
    g = jnp.where(row < PAIRS, g, 0.0)
    gcol = g[:, 0:1]
    sr = gr_ref[...] * gcol
    sr_ref[...] = sr
    sq = (gq_ref[...] * gcol).astype(BF16)
    sq_ref[...] = sq
    srb = sr.astype(BF16)
    for gkv_ref, s_ref in ((gkva_ref, skva_ref), (gkvb_ref, skvb_ref)):
        for p in range(PAIRS):
            rows = slice(p * SEQ, (p + 1) * SEQ)
            s_ref[rows, :] = (gkv_ref[rows, :] * gcol[p : p + 1, :]).astype(BF16)
    for half, out_ref, s_ref in ((1, grad_b_ref, skvb_ref), (0, grad_a_ref, skva_ref)):
        cols = slice(half * 512, half * 512 + 512)
        out_ref[:, 0:512] = dot(turned_ref[...], s_ref[...]).astype(BF16)
        out_ref[:, 512:1024] = dot(nlast_ref[...], sq[:, cols], FIRST).astype(BF16)
        out_ref[:, 1024:1536] = dot(srb, ctx_ref[:, cols], FIRST).astype(BF16)


def hidden_body(
    len_ref, h_ref, gain_ref, wa_ref, wb_ref, skva_ref, skvb_ref, sq_ref, sr_ref, out_ref, last_scr
):
    last_scr[...] = dot(sq_ref[:, 0:512], wa_ref[:, 512:1024], LAST) + dot(
        sq_ref[:, 512:1024], wb_ref[:, 512:1024], LAST
    )
    pos = lax.broadcasted_iota(jnp.int32, (SEQ, 1), 0)
    for p in range(PAIRS):
        rows = slice(p * SEQ, (p + 1) * SEQ)
        gn = dot(skva_ref[rows, :], wa_ref[:, 0:512], LAST) + dot(
            skvb_ref[rows, :], wb_ref[:, 0:512], LAST
        )
        at = pos == len_ref[p] - 1
        gn = gn + jnp.where(at, last_scr[p : p + 1, :], 0.0)
        x = h_ref[rows, :].astype(F32)
        inv = lax.rsqrt(jnp.mean(x * x, axis=-1, keepdims=True) + EPS)
        s = gn * gain_ref[...]
        gi = inv * s - x * (inv * inv * inv * jnp.mean(s * x, axis=-1, keepdims=True))
        gi = gi + jnp.where(at, sr_ref[p : p + 1, :], 0.0)
        out_ref[rows, :] = gi.astype(BF16)


def everyone(x, axes, count):
    return lax.all_to_all(
        jnp.broadcast_to(x[None], (count, *x.shape)), axes, 0, 0, tiled=True
    )


def gather_rows(x):
    width = x.shape[1]
    got = everyone(x, ("z", "x"), 32).reshape(256, width)
    return everyone(got, "pb", 4).reshape(1024, width)


def scatter_rows(x):
    width = x.shape[1]
    got = lax.all_to_all(x.reshape(4, 256, width), "pb", 0, 0, tiled=True)
    part = jnp.sum(got.astype(F32), axis=0).astype(BF16)
    got = lax.all_to_all(part.reshape(32, 8, width), ("z", "x"), 0, 0, tiled=True)
    return jnp.sum(got.astype(F32), axis=0)


def swap(x):
    return lax.ppermute(x, "c", [(0, 1), (1, 0)])


def shards(
    hidden,
    lengths,
    teacher,
    norm_gain,
    final_gain,
    score_vector,
    query_weight,
    key_matrix,
    value_matrix,
    out_weight,
):
    c = lax.axis_index("c")
    first = c == 0
    pb = lax.axis_index("pb").astype(jnp.int32)[None]
    tokens = hidden.reshape(ROWS, D)
    lens = lengths[0]
    gain = norm_gain[None]
    fg = final_gain[None]
    sv = score_vector[None]
    cos_np, sin_np = rope_consts()
    cos, sin = jnp.asarray(cos_np), jnp.asarray(sin_np)
    teach = jnp.broadcast_to(jnp.pad(teacher[0], (0, 4))[:, None], (8, HW))

    turned_out = out_weight.T
    halves = [
        jnp.concatenate(
            [
                key_matrix[:, h * 256 : h * 256 + 256],
                value_matrix[:, h * 256 : h * 256 + 256],
                query_weight[:, h * 512 : h * 512 + 512],
                turned_out[:, h * 512 : h * 512 + 512],
            ],
            axis=1,
        )
        for h in range(2)
    ]
    mine = jnp.where(first, halves[0], halves[1])
    theirs = swap(jnp.where(first, halves[1], halves[0]))
    block = jnp.concatenate(
        [jnp.where(first, mine, theirs), jnp.where(first, theirs, mine)], axis=0
    )
    wa = gather_rows(block[:, 0:1024])
    oa = gather_rows(block[:, 1024:1536])
    wb = swap(wa)
    ob = swap(oa)

    normed, turned, nlast, xlast = call(
        prep_body,
        [((ROWS, D), BF16), ((D, ROWS), BF16), ((8, D), BF16), ((8, D), F32)],
        [SM, VM, VM],
        flops=10_000_000,
        nbytes=4 << 20,
    )(lens, tokens, gain)

    kproj, krot, vcast, qproj, qrot, attn, ctx = pl.pallas_call(
        attend_body,
        out_shape=[
            jax.ShapeDtypeStruct((ROWS, 512), F32),
            jax.ShapeDtypeStruct((ROWS, 512), BF16),
            jax.ShapeDtypeStruct((ROWS, 512), BF16),
            jax.ShapeDtypeStruct((8, D), F32),
            jax.ShapeDtypeStruct((8, D), BF16),
            jax.ShapeDtypeStruct((32, SEQ), F32),
            jax.ShapeDtypeStruct((8, D), BF16),
        ],
        in_specs=[SM] + [VM] * 6,
        out_specs=[VM] * 7,
        scratch_shapes=[pltpu.VMEM((8, D), F32), pltpu.VMEM((8, D), F32)],
        compiler_params=pltpu.CompilerParams(vmem_limit_bytes=48 << 20),
        cost_estimate=pl.CostEstimate(
            flops=1_100_000_000, bytes_accessed=8 << 20, transcendentals=0
        ),
    )(lens, normed, nlast, wa, wb, cos, sin)

    unit, oscale, score, tot = call(
        score_body,
        [((8, D), F32), ((8, HW), F32), ((8, HW), F32), ((8, HW), F32)],
        [VM] * 7,
        flops=20_000_000,
        nbytes=2 << 20,
    )(teach, ctx, xlast, oa, ob, fg, sv)

    totals = everyone(tot[0:1], AXES, 256).reshape(256, HW)

    gkva, gkvb, gq, gr = pl.pallas_call(
        unit_back_body,
        out_shape=[
            jax.ShapeDtypeStruct((ROWS, 512), F32),
            jax.ShapeDtypeStruct((ROWS, 512), F32),
            jax.ShapeDtypeStruct((8, D), F32),
            jax.ShapeDtypeStruct((8, D), F32),
        ],
        in_specs=[SM] + [VM] * 14,
        out_specs=[VM] * 4,
        scratch_shapes=[pltpu.VMEM((8, D), F32)] * 3,
        compiler_params=pltpu.CompilerParams(vmem_limit_bytes=48 << 20),
        cost_estimate=pl.CostEstimate(
            flops=200_000_000, bytes_accessed=8 << 20, transcendentals=0
        ),
    )(lens, krot, vcast, kproj, qproj, qrot, attn, unit, oscale, oa, ob, fg, sv, cos, sin)

    loss, grad_a, grad_b, skva, skvb, sq, sr = call(
        weight_body,
        [
            ((8, HW), F32),
            ((D, 1536), BF16),
            ((D, 1536), BF16),
            ((ROWS, 512), BF16),
            ((ROWS, 512), BF16),
            ((8, D), BF16),
            ((8, D), F32),
        ],
        [SM] + [VM] * 10,
        flops=1_100_000_000,
        nbytes=12 << 20,
    )(pb, totals, score, teach, gkva, gkvb, gq, gr, turned, nlast, ctx)

    other = swap(grad_b)
    chip = (grad_a.astype(F32) + other.astype(F32)).astype(BF16)
    reduced = scatter_rows(chip)

    (grad_hidden,) = pl.pallas_call(
        hidden_body,
        out_shape=[jax.ShapeDtypeStruct((ROWS, D), BF16)],
        in_specs=[SM] + [VM] * 8,
        out_specs=[VM],
        scratch_shapes=[pltpu.VMEM((8, D), F32)],
        compiler_params=pltpu.CompilerParams(vmem_limit_bytes=48 << 20),
        cost_estimate=pl.CostEstimate(
            flops=1_100_000_000, bytes_accessed=8 << 20, transcendentals=0
        ),
    )(lens, tokens, gain, wa, wb, skva, skvb, sq, sr)

    keep = jnp.where(first, reduced[0:4], reduced[4:8])
    got = swap(jnp.where(first, reduced[4:8], reduced[0:4]))
    low = jnp.where(first, keep, got)
    high = jnp.where(first, got, keep)

    def both(a, b):
        return jnp.concatenate([low[:, a:b], high[:, a:b]], axis=1)

    return (
        score[0:PAIRS, 0][None],
        loss[0, 0],
        grad_hidden.reshape(hidden.shape),
        both(512, 1024),
        both(0, 256),
        both(256, 512),
        both(1024, 1536).T,
    )


def solution(mesh):
    torus = Mesh(mesh.devices.reshape(mesh.shape["pb"], 8, 4, 2), AXES)
    placed = (
        P("pb", NEG, None, None),
        P("pb", NEG),
        P("pb", NEG),
        P(),
        P(),
        P(),
        P(AXES, None),
        P(AXES, None),
        P(AXES, None),
        P(None, AXES),
    )
    return jax.shard_map(
        shards,
        mesh=torus,
        in_specs=placed,
        out_specs=(
            P("pb", NEG),
            P(),
            P("pb", NEG, None, None),
            P(AXES, None),
            P(AXES, None),
            P(AXES, None),
            P(None, AXES),
        ),
        check_vma=False,
    )
```

time: 433 us -> 239 us (0.55)
  waiting for transfers between devices: 264 us -> 59.1 us
  starting transfers between devices: 0.34 us -> 39.9 us
  matrix products: 26.8 us -> 0 us
  Pallas kernels: 0 us -> 22.2 us
  blocking collectives: 58.6 us -> 80.1 us
  local copies, waits for them, and re-layouts: 40 us -> 25.1 us
  between operations: 15.6 us -> 0.93 us
  other arithmetic: 22.8 us -> 10.2 us
    reduce_scatter x3 -> x0, waiting for transfers between devices: 148 us -> none  [the longest x1 83.9 us: sum_packed(): lax.psum_scatter(lines, axis, tiled=True).reshape(-1)]
    all_gather x1 -> x0, waiting for transfers between devices: 116 us -> none  [gather_turned(): out, at, outs = (lax.all_gather(both, axis, axis=0, tiled=True), 0, [])]
    all_to_all x1 -> x3, blocking collectives: 17 us -> 80.1 us  [the longest x1 40.7 us: scatter_rows(): got = lax.all_to_all(x.reshape(4, 256, width), 'pb', 0, 0, tiled=True)]
    all_to_all x0 -> x4, waiting for transfers between devices: none -> 52.7 us  [the longest x3 33.6 us: everyone(): lax.all_to_all(jnp.broadcast_to(x[None], (count, *x.shape)), axes, 0, 0,...]
    psum x4 -> x0, blocking collectives: 41.6 us -> none  [one_axis_at_a_time(): shard = lax.psum(shard, axis)]
    dot_general x20 -> x0, matrix products: 26.8 us -> none  [the longest x1 3.18 us: forward_pairs(): jnp.dot(flat_rows, value_matrix, preferred_element_type=jnp.float32)]
    all_to_all x0 -> x4, starting transfers between devices: none -> 24.8 us  [the longest x3 16 us: everyone(): lax.all_to_all(jnp.broadcast_to(x[None], (count, *x.shape)), axes, 0, 0,...]
    pallas_call x0 -> x6, Pallas kernels: none -> 22.2 us  [the longest x1 6.45 us: shards(): pl.pallas_call(hidden_body, out_shape=[jax.ShapeDtypeStruct((ROWS, D), BF...]
  transfers between devices with their start and end apart: 4 -> 9, of which waited for: 4 -> 6; matrix products, arithmetic and copies ran while one was open for 7% -> 1% of each run, Pallas kernels for 0% -> 7%
where the time goes in v1:
time: 239 us; the launch traced here: 238 us
  blocking collectives  80.1 us (34%)
  waiting for transfers between devices  59.1 us (25%)
  starting transfers between devices  39.9 us (17%)
  local copies, waits for them, and re-layouts  25.1 us (11%)
  Pallas kernels  22.2 us (9%)
  other arithmetic  10.2 us (4%)
    all_to_all x1, blocking collectives, scatter_rows(): got = lax.all_to_all(x.reshape(4, 256, width), 'pb', 0, 0, tiled=True)  40.7 us
    all_to_all x2, blocking collectives, everyone(): lax.all_to_all(jnp.broadcast_to(x[None], (count, *x.shape)), axes, 0, 0,...  39.5 us
    all_to_all x3, waiting for transfers between devices, everyone(): lax.all_to_all(jnp.broadcast_to(x[None], (count, *x.shape)), axes, 0, 0,...  33.6 us
    unnamed x72, local copies, waits for them, and re-layouts  19.2 us
    all_to_all x1, waiting for transfers between devices, scatter_rows(): lax.all_to_all(part.reshape(32, 8, width), ('z', 'x'), 0, 0, tiled=True)  19.1 us
    all_to_all x3, starting transfers between devices, everyone(): lax.all_to_all(jnp.broadcast_to(x[None], (count, *x.shape)), axes, 0, 0,...  16 us
    ppermute x5, starting transfers between devices, swap(): return lax.ppermute(x, 'c', [(0, 1), (1, 0)])  15.1 us
    all_to_all x1, starting transfers between devices, scatter_rows(): lax.all_to_all(part.reshape(32, 8, width), ('z', 'x'), 0, 0, tiled=True)  8.73 us
  transfers between devices with their start and end apart: 9, of which 6 were waited for; matrix products, arithmetic and copies ran while one was open for 1% of the time, Pallas kernels for 7%

profile of v1, /device:TPU:1, one launch (start us, length us, event | category | flops | bytes accessed | tf_op | source)
XLA Modules:
  0.0 237.5 jit_solution(2293571653293754073)
XLA Ops:
  2.1 3.3 %collective-permute-start = (bf16[4,1536]{1,0:T(4,128)(2,1)S(1)}, bf16[4,1536]{1,0:T(4,128)(2,1)S(1)}, u32[]{:S(2)}, u32[]{:S(2)}) collective-permute-start(bf16[4,1536]{1,0:T(4,128)(2,1)S(1)} %broadcast_select_fusion.4), channel_id=1, source_target_pairs={{0,1},{1,0},{2,3},{3,2},{4,5},{5,4},{6,7},{7,6},{8,9},{9,8},{10,11... | collective-permute-start | bytes 36872 | tf_op jit(solution)/shard_map/ppermute | solution.py:354
  6.4 25.7 %all_to_all.35 = bf16[32,8,1024]{2,1,0:T(8,128)(2,1)S(1)} all-to-all(bf16[32,8,1024]{2,1,0:T(8,128)(2,1)S(1)} %broadcast_in_dim.54), channel_id=1, replica_groups=mesh['pb'=4,'z'=8,'x'=4,'c'=2] {'z','x'}, dimensions={0} | all-to-all | bytes 1048576 | tf_op jit(solution)/shard_map/all_to_all | solution.py:334
  32.1 1.6 broadcast_in_dim.56
  33.7 4.2 %all-to-all-start.1 = ((bf16[4,256,1024]{2,1,0:T(8,128)(2,1)}), bf16[4,256,1024]{2,1,0:T(8,128)(2,1)S(1)}, u32[]{:S(2)}, u32[]{:S(2)}) async-start(bf16[4,256,1024]{2,1,0:T(8,128)(2,1)} %broadcast_in_dim.56), calls=%async_computation.1 | async-start | bytes 4194304 | tf_op jit(solution)/shard_map/all_to_all | solution.py:334
  37.9 23.8 %all-to-all-done.1 = bf16[4,256,1024]{2,1,0:T(8,128)(2,1)S(1)} async-done(((bf16[4,256,1024]{2,1,0:T(8,128)(2,1)}), bf16[4,256,1024]{2,1,0:T(8,128)(2,1)S(1)}, u32[]{:S(2)}, u32[]{:S(2)}) %all-to-all-start.1) | async-done | bytes 2097184 | tf_op jit(solution)/shard_map/all_to_all | solution.py:334
  62.5 6.7 %all-to-all-start.2 = ((bf16[32,8,512]{2,1,0:T(8,128)(2,1)}), bf16[32,8,512]{2,1,0:T(8,128)(2,1)S(1)}, u32[]{:S(2)}, u32[]{:S(2)}) async-start(bf16[32,8,512]{2,1,0:T(8,128)(2,1)} %broadcast_in_dim.57), calls=%async_computation.2 | async-start | bytes 524288 | tf_op jit(solution)/shard_map/all_to_all | solution.py:334
  69.1 2.1 collective-permute-start.1
  71.3 8.3 %all-to-all-done.2 = bf16[32,8,512]{2,1,0:T(8,128)(2,1)S(1)} async-done(((bf16[32,8,512]{2,1,0:T(8,128)(2,1)}), bf16[32,8,512]{2,1,0:T(8,128)(2,1)S(1)}, u32[]{:S(2)}, u32[]{:S(2)}) %all-to-all-start.2) | async-done | bytes 262176 | tf_op jit(solution)/shard_map/all_to_all | solution.py:334
  79.6 13.8 %all_to_all.36 = bf16[4,256,512]{2,1,0:T(8,128)(2,1)S(1)} all-to-all(bf16[4,256,512]{2,1,0:T(8,128)(2,1)S(1)} %broadcast_in_dim.59), channel_id=1, replica_groups=mesh['pb'=4,'z'=8,'x'=4,'c'=2] {'pb'}, dimensions={0} | all-to-all | bytes 2097152 | tf_op jit(solution)/shard_map/all_to_all | solution.py:334
  93.4 4.7 %collective-permute-start.2 = (bf16[1024,512]{1,0:T(8,128)(2,1)S(1)}, bf16[1024,512]{1,0:T(8,128)(2,1)S(1)}, u32[]{:S(2)}, u32[]{:S(2)}) collective-permute-start(bf16[1024,512]{1,0:T(8,128)(2,1)S(1)} %bitcast.25), channel_id=1, source_target_pairs={{0,1},{1,0},{2,3},{3,2},{4,5},{5,4},{6,7},{7,6},{8,9},{9,8},{10,11... | collective-permute-start | bytes 3145736 | tf_op jit(solution)/shard_map/ppermute | solution.py:354
  99.4 1.3 shard_map.171
  100.7 5.1 %shard_map.172 = (f32[512,512]{1,0:T(8,128)S(1)}, bf16[512,512]{1,0:T(8,128)(2,1)S(1)}, bf16[512,512]{1,0:T(8,128)(2,1)S(1)}, f32[8,1024]{1,0:T(8,128)S(1)}, bf1...) custom-call(s32[4]{0:T(128)S(1)} %bitcast.38, ...), custom_call_target="tpu_custom_call" | custom-call | flops 1100000000 | bytes 8388608 | tf_op jit(solution)/shard_map/pallas_call | solution.py:412
  109.6 5.2 %all-to-all-start.4 = ((f32[256,1,128]{2,1,0:T(1,128)}), f32[256,1,128]{2,1,0:T(1,128)S(1)}, u32[]{:S(2)}, u32[]{:S(2)}) async-start(f32[256,1,128]{2,1,0:T(1,128)} %broadcast_in_dim.64), calls=%async_computation.4 | async-start | bytes 262144 | tf_op jit(solution)/shard_map/all_to_all | solution.py:334
  119.5 3.5 %shard_map.174 = (f32[512,512]{1,0:T(8,128)S(1)}, f32[512,512]{1,0:T(8,128)S(1)}, f32[8,1024]{1,0:T(8,128)S(1)}, f32[8,1024]{1,0:T(8,128)S(1)}) custom-call(s32[4]{0:T(128)S(1)} %bitcast.39, bf16[512,512]{1,0:T(8,128)(2,1)S(1)} %copy-done.10, bf16[512,512]{1,0:T(8,128)(2,1)S(1)} %copy-done.12, f32[512,512]{1,0:T(8,128)S(1)} %copy-done.4, ...), custom_call_target="tpu_custom_call" | custom-call | flops 200000000 | bytes 8388608 | tf_op jit(solution)/shard_map/pallas_call | solution.py:442
  126.1 1.5 all-to-all-done.4
  133.5 5.1 %shard_map.175 = (f32[8,128]{1,0:T(8,128)S(1)}, bf16[1024,1536]{1,0:T(8,128)(2,1)}, bf16[1024,1536]{1,0:T(8,128)(2,1)}, bf16[512,512]{1,0:T(8,128)(2,1)S(1)}, bf...) custom-call(s32[1]{0:T(128)} %bitcast.11.pb_ref, f32[256,128]{1,0:T(8,128)S(1)} %bitcast.30, ...), custom_call_target="tpu_custom_call" | custom-call | flops 1100000000 | bytes 12582912 | tf_op jit(solution)/shard_map/pallas_call | solution.py:459
  139.3 5.5 %collective-permute-done.3 = bf16[1024,1536]{1,0:T(8,128)(2,1)S(1)} collective-permute-done((bf16[1024,1536]{1,0:T(8,128)(2,1)}, bf16[1024,1536]{1,0:T(8,128)(2,1)S(1)}, u32[]{:S(2)}, u32[]{:S(2)}) %collective-permute-start.3) | collective-permute-done | bytes 3145760 | tf_op jit(solution)/shard_map/ppermute | solution.py:354
  144.8 2.9 %add_convert_fusion = bf16[1024,1536]{1,0:T(8,128)(2,1)S(1)} fusion(bf16[1024,1536]{1,0:T(8,128)(2,1)S(1)} %collective-permute-done.3, bf16[1024,1536]{1,0:T(8,128)(2,1)} %get-tuple-element.57), kind=kLoop, calls=%fused_computation | loop fusion | flops 6291456 | bytes 9437184 | tf_op jit(solution)/shard_map/convert_element_type | solution.py:476
  147.7 40.7 %all_to_all.37 = bf16[4,256,1536]{2,1,0:T(8,128)(2,1)} all-to-all(bf16[4,256,1536]{2,1,0:T(8,128)(2,1)S(1)} %bitcast.41), channel_id=1, replica_groups=mesh['pb'=4,'z'=8,'x'=4,'c'=2] {'pb'}, dimensions={0} | all-to-all | bytes 6291456 | tf_op jit(solution)/shard_map/all_to_all | solution.py:347
  188.4 3.5 %reduce_sum.21 = bf16[256,1536]{1,0:T(8,128)(2,1)} reduce(bf16[4,256,1536]{2,1,0:T(8,128)(2,1)} %all_to_all.37, bf16[]{:T(256)} %constant.20.clone.1), dimensions={0}, to_apply=%region_0.1 | reduce | flops 1179648 | bytes 3932162 | tf_op jit(solution)/shard_map/reduce_sum | solution.py:348
  191.9 8.7 %all-to-all-start.6 = ((bf16[32,8,1536]{2,1,0:T(8,128)(2,1)}), bf16[32,8,1536]{2,1,0:T(8,128)(2,1)}, u32[]{:S(2)}, u32[]{:S(2)}) async-start(bf16[32,8,1536]{2,1,0:T(8,128)(2,1)} %bitcast.42), calls=%async_computation.6 | async-start | bytes 1572864 | tf_op jit(solution)/shard_map/all_to_all | solution.py:349
  201.2 19.1 %all-to-all-done.6 = bf16[32,8,1536]{2,1,0:T(8,128)(2,1)} async-done(((bf16[32,8,1536]{2,1,0:T(8,128)(2,1)}), bf16[32,8,1536]{2,1,0:T(8,128)(2,1)}, u32[]{:S(2)}, u32[]{:S(2)}) %all-to-all-start.6) | async-done | bytes 786464 | tf_op jit(solution)/shard_map/all_to_all | solution.py:349
  221.6 4.3 %collective-permute-start.4 = (f32[4,1536]{1,0:T(4,128)S(1)}, f32[4,1536]{1,0:T(4,128)S(1)}, u32[]{:S(2)}, u32[]{:S(2)}) collective-permute-start(f32[4,1536]{1,0:T(4,128)S(1)} %slice_select_fusion), channel_id=1, source_target_pairs={{0,1},{1,0},{2,3},{3,2},{4,5},{5,4},{6,7},{7,6},{8,9},{9,8},{10,11... | collective-permute-start | bytes 73736 | tf_op jit(solution)/shard_map/ppermute | solution.py:354
  228.1 6.4 %shard_map.176 = bf16[512,1024]{1,0:T(8,128)(2,1)} custom-call(s32[4]{0:T(128)S(1)} %bitcast.40, bf16[512,1024]{1,0:T(8,128)(2,1)S(1)} %bitcast.29, f32[1,1024]{1,0:T(1,128)S(1)} %bitcast.32, bf16[1024,1024]{1,0:T(8,128)(2,1)S(1)} %bitcast.24, bf16[1024,1024]{1,0:T(8,128)(2,1)} %collective-permute-done.1.wb_ref, bf16[512,512]{1,0:T(8,128)(2,1)S(1)} %copy-done.6, ...), custom_call_target="tpu_custom_call" | custom-call | flops 1100000000 | bytes 8388608 | tf_op jit(solution)/shard_map/pallas_call | solution.py:479
  (104 shorter events, 29.5 us)
Async XLA Ops:
  2.1 4.2 %collective-permute-start = (bf16[4,1536]{1,0:T(4,128)(2,1)S(1)}, bf16[4,1536]{1,0:T(4,128)(2,1)S(1)}, u32[]{:S(2)}, u32[]{:S(2)}) collective-permute-start(bf16[4,1536]{1,0:T(4,128)(2,1)S(1)} %broadcast_select_fusion.4), channel_id=1, source_target_pairs={{0,1},{1,0},{2,3},{3,2},{4,5},{5,4},{6,7},{7,6},{8,9},{9,8},{10,11... | collective-permute-start | bytes 36872 | tf_op jit(solution)/shard_map/ppermute | solution.py:354
  33.7 28.1 %all-to-all-start.1 = ((bf16[4,256,1024]{2,1,0:T(8,128)(2,1)}), bf16[4,256,1024]{2,1,0:T(8,128)(2,1)S(1)}, u32[]{:S(2)}, u32[]{:S(2)}) async-start(bf16[4,256,1024]{2,1,0:T(8,128)(2,1)} %broadcast_in_dim.56), calls=%async_computation.1 | async-start | bytes 4194304 | tf_op jit(solution)/shard_map/all_to_all | solution.py:334
  37.9 60.2 %copy-start.35 = (f32[1,4]{1,0:T(1,128)S(1)}, f32[1,4]{1,0:T(1,128)}, u32[]{:S(2)}) copy-start(f32[1,4]{1,0:T(1,128)} %param.14) | copy-start | bytes 52
  37.9 60.3 %copy-start.15 = (f32[1024]{0:T(1024)S(1)}, f32[1024]{0:T(1024)}, u32[]{:S(2)}) copy-start(f32[1024]{0:T(1024)} %param.15) | copy-start | bytes 12292
  37.9 60.3 %copy-start.18 = (s32[1,4]{1,0:T(1,128)S(1)}, s32[1,4]{1,0:T(1,128)}, u32[]{:S(2)}) copy-start(s32[1,4]{1,0:T(1,128)} %param.13) | copy-start | bytes 52
  37.9 62.8 %copy-start.13 = (f32[128,128]{1,0:T(8,128)S(1)}, f32[128,128]{1,0:T(8,128)}, u32[]{:S(2)}) copy-start(f32[128,128]{1,0:T(8,128)} %constant.21.clone.cos_ref) | copy-start | bytes 196612
  37.9 62.8 %copy-start.14 = (f32[128,128]{1,0:T(8,128)S(1)}, f32[128,128]{1,0:T(8,128)}, u32[]{:S(2)}) copy-start(f32[128,128]{1,0:T(8,128)} %constant.22.clone.sin_ref) | copy-start | bytes 196612
  62.5 17.1 %all-to-all-start.2 = ((bf16[32,8,512]{2,1,0:T(8,128)(2,1)}), bf16[32,8,512]{2,1,0:T(8,128)(2,1)S(1)}, u32[]{:S(2)}, u32[]{:S(2)}) async-start(bf16[32,8,512]{2,1,0:T(8,128)(2,1)} %broadcast_in_dim.57), calls=%async_computation.2 | async-start | bytes 524288 | tf_op jit(solution)/shard_map/all_to_all | solution.py:334
  69.1 31.5 %collective-permute-start.1 = (bf16[1024,1024]{1,0:T(8,128)(2,1)S(1)}, bf16[1024,1024]{1,0:T(8,128)(2,1)}, u32[]{:S(2)}, u32[]{:S(2)}) collective-permute-start(bf16[1024,1024]{1,0:T(8,128)(2,1)S(1)} %bitcast.22), channel_id=1, source_target_pairs={{0,1},{1,0},{2,3},{3,2},{4,5},{5,4},{6,7},{7,6},{8,9},{9,8},{10,11... | collective-permute-start | bytes 6291464 | tf_op jit(solution)/shard_map/ppermute | solution.py:354
  93.4 12.4 %collective-permute-start.2 = (bf16[1024,512]{1,0:T(8,128)(2,1)S(1)}, bf16[1024,512]{1,0:T(8,128)(2,1)S(1)}, u32[]{:S(2)}, u32[]{:S(2)}) collective-permute-start(bf16[1024,512]{1,0:T(8,128)(2,1)S(1)} %bitcast.25), channel_id=1, source_target_pairs={{0,1},{1,0},{2,3},{3,2},{4,5},{5,4},{6,7},{7,6},{8,9},{9,8},{10,11... | collective-permute-start | bytes 3145736 | tf_op jit(solution)/shard_map/ppermute | solution.py:354
  98.1 1.2 copy-start
  99.4 6.5 %copy-start.16 = (f32[1024]{0:T(1024)S(1)}, f32[1024]{0:T(1024)}, u32[]{:S(2)}) copy-start(f32[1024]{0:T(1024)} %param.16) | copy-start | bytes 12292
  99.4 6.5 %copy-start.17 = (f32[1024]{0:T(1024)S(1)}, f32[1024]{0:T(1024)}, u32[]{:S(2)}) copy-start(f32[1024]{0:T(1024)} %param.17) | copy-start | bytes 12292
  100.6 6.1 %copy-start.25 = (bf16[1024,512]{1,0:T(8,128)(2,1)}, bf16[1024,512]{1,0:T(8,128)(2,1)S(1)}, u32[]{:S(2)}) copy-start(bf16[1024,512]{1,0:T(8,128)(2,1)S(1)} %get-tuple-element.51.turned_ref) | copy-start | bytes 3145732
  105.8 3.1 %copy-start.9 = (bf16[512,512]{1,0:T(8,128)(2,1)}, bf16[512,512]{1,0:T(8,128)(2,1)S(1)}, u32[]{:S(2)}) copy-start(bf16[512,512]{1,0:T(8,128)(2,1)S(1)} %get-tuple-element.39.krot_ref) | copy-start | bytes 1572868
  105.8 3.1 %copy-start.11 = (bf16[512,512]{1,0:T(8,128)(2,1)}, bf16[512,512]{1,0:T(8,128)(2,1)S(1)}, u32[]{:S(2)}) copy-start(bf16[512,512]{1,0:T(8,128)(2,1)S(1)} %get-tuple-element.40.vcast_ref) | copy-start | bytes 1572868
  109.6 18.0 %all-to-all-start.4 = ((f32[256,1,128]{2,1,0:T(1,128)}), f32[256,1,128]{2,1,0:T(1,128)S(1)}, u32[]{:S(2)}, u32[]{:S(2)}) async-start(f32[256,1,128]{2,1,0:T(1,128)} %broadcast_in_dim.64), calls=%async_computation.4 | async-start | bytes 262144 | tf_op jit(solution)/shard_map/all_to_all | solution.py:334
  138.6 9.1 %copy-start.5 = (bf16[512,512]{1,0:T(8,128)(2,1)}, bf16[512,512]{1,0:T(8,128)(2,1)S(1)}, u32[]{:S(2)}) copy-start(bf16[512,512]{1,0:T(8,128)(2,1)S(1)} %get-tuple-element.53.skva_ref) | copy-start | bytes 1572868
  138.6 9.1 %copy-start.7 = (bf16[512,512]{1,0:T(8,128)(2,1)}, bf16[512,512]{1,0:T(8,128)(2,1)S(1)}, u32[]{:S(2)}) copy-start(bf16[512,512]{1,0:T(8,128)(2,1)S(1)} %get-tuple-element.54.skvb_ref) | copy-start | bytes 1572868
  138.6 6.1 %collective-permute-start.3 = (bf16[1024,1536]{1,0:T(8,128)(2,1)}, bf16[1024,1536]{1,0:T(8,128)(2,1)S(1)}, u32[]{:S(2)}, u32[]{:S(2)}) collective-permute-start(bf16[1024,1536]{1,0:T(8,128)(2,1)} %get-tuple-element.58), channel_id=1, source_target_pairs={{0,1},{1,0},{2,3},{3,2},{4,5},{5,4},{6,7},{7,6},{8,9},{9,8},{10,11... | collective-permute-start | bytes 9437192 | tf_op jit(solution)/shard_map/ppermute | solution.py:354
  188.3 37.6 %copy-start.1 = (bf16[1,4,128,1024]{3,2,1,0:T(8,128)(2,1)S(1)}, bf16[1,4,128,1024]{3,2,1,0:T(8,128)(2,1)}, u32[]{:S(2)}) copy-start(bf16[1,4,128,1024]{3,2,1,0:T(8,128)(2,1)} %param.12) | copy-start | bytes 3145732
  188.4 37.6 %copy-start.20 = (s32[1,4]{1,0:T(1,128)S(1)}, s32[1,4]{1,0:T(1,128)}, u32[]{:S(2)}) copy-start(s32[1,4]{1,0:T(1,128)} %param.13) | copy-start | bytes 52
  191.9 28.5 %all-to-all-start.6 = ((bf16[32,8,1536]{2,1,0:T(8,128)(2,1)}), bf16[32,8,1536]{2,1,0:T(8,128)(2,1)}, u32[]{:S(2)}, u32[]{:S(2)}) async-start(bf16[32,8,1536]{2,1,0:T(8,128)(2,1)} %bitcast.42), calls=%async_computation.6 | async-start | bytes 1572864 | tf_op jit(solution)/shard_map/all_to_all | solution.py:349
  221.6 13.4 %collective-permute-start.4 = (f32[4,1536]{1,0:T(4,128)S(1)}, f32[4,1536]{1,0:T(4,128)S(1)}, u32[]{:S(2)}, u32[]{:S(2)}) collective-permute-start(f32[4,1536]{1,0:T(4,128)S(1)} %slice_select_fusion), channel_id=1, source_target_pairs={{0,1},{1,0},{2,3},{3,2},{4,5},{5,4},{6,7},{7,6},{8,9},{9,8},{10,11... | collective-permute-start | bytes 73736 | tf_op jit(solution)/shard_map/ppermute | solution.py:354
  (21 other events, 18.9 us)

commit v2 on v1

--- a/solution.py
+++ b/solution.py
@@ -37,7 +37,7 @@
     )
 
 
-def call(body, outs, in_specs, vmem=48, flops=0, nbytes=0):
+def call(body, outs, in_specs, vmem=24, flops=0, nbytes=0):
     return pl.pallas_call(
         body,
         out_shape=[jax.ShapeDtypeStruct(s, d) for s, d in outs],
@@ -106,8 +106,10 @@
     len_ref,
     normed_ref,
     nlast_ref,
-    wa_ref,
-    wb_ref,
+    kva_ref,
+    kvb_ref,
+    qa_ref,
+    qb_ref,
     cos_ref,
     sin_ref,
     kproj_ref,
@@ -122,11 +124,11 @@
 ):
     mask, even = block_mask()
     lane = lax.broadcasted_iota(jnp.int32, (8, SEQ), 1)
-    for half, w_ref in enumerate((wa_ref, wb_ref)):
-        kv = dot(normed_ref[...], w_ref[:, 0:512])
+    for half, (kv_ref, q_ref) in enumerate(((kva_ref, qa_ref), (kvb_ref, qb_ref))):
+        kv = dot(normed_ref[...], kv_ref[...])
         kproj_ref[:, half * 256 : half * 256 + 256] = kv[:, 0:256]
         vcast_ref[:, half * 256 : half * 256 + 256] = kv[:, 256:512].astype(BF16)
-        qproj_ref[:, half * 512 : half * 512 + 512] = dot(nlast_ref[...], w_ref[:, 512:1024])
+        qproj_ref[:, half * 512 : half * 512 + 512] = dot(nlast_ref[...], q_ref[...])
     cos_q = jnp.concatenate(
         [cos_ref[pl.ds(len_ref[p] - 1, 1), :] for p in range(PAIRS)] * 2, axis=0
     )
@@ -266,8 +268,9 @@
     nlast_ref,
     ctx_ref,
     loss_ref,
-    grad_a_ref,
-    grad_b_ref,
+    grad_kvb_ref,
+    grad_qb_ref,
+    grad_ob_ref,
     skva_ref,
     skvb_ref,
     sq_ref,
@@ -296,29 +299,46 @@
     sr_ref[...] = sr
     sq = (gq_ref[...] * gcol).astype(BF16)
     sq_ref[...] = sq
-    srb = sr.astype(BF16)
-    for gkv_ref, s_ref in ((gkva_ref, skva_ref), (gkvb_ref, skvb_ref)):
+    for gkv_ref, s_ref in ((gkvb_ref, skvb_ref), (gkva_ref, skva_ref)):
         for p in range(PAIRS):
             rows = slice(p * SEQ, (p + 1) * SEQ)
             s_ref[rows, :] = (gkv_ref[rows, :] * gcol[p : p + 1, :]).astype(BF16)
-    for half, out_ref, s_ref in ((1, grad_b_ref, skvb_ref), (0, grad_a_ref, skva_ref)):
-        cols = slice(half * 512, half * 512 + 512)
-        out_ref[:, 0:512] = dot(turned_ref[...], s_ref[...]).astype(BF16)
-        out_ref[:, 512:1024] = dot(nlast_ref[...], sq[:, cols], FIRST).astype(BF16)
-        out_ref[:, 1024:1536] = dot(srb, ctx_ref[:, cols], FIRST).astype(BF16)
+    grad_kvb_ref[...] = dot(turned_ref[...], skvb_ref[...]).astype(BF16)
+    grad_qb_ref[...] = dot(nlast_ref[...], sq[:, 512:1024], FIRST).astype(BF16)
+    grad_ob_ref[...] = dot(sr.astype(BF16), ctx_ref[:, 512:1024], FIRST).astype(BF16)
+
+
+def own_weight_body(
+    skva_ref, sq_ref, sr_ref, turned_ref, nlast_ref, ctx_ref, grad_kva_ref, grad_qa_ref, grad_oa_ref
+):
+    grad_kva_ref[...] = dot(turned_ref[...], skva_ref[...]).astype(BF16)
+    grad_qa_ref[...] = dot(nlast_ref[...], sq_ref[:, 0:512], FIRST).astype(BF16)
+    grad_oa_ref[...] = dot(sr_ref[...].astype(BF16), ctx_ref[:, 0:512], FIRST).astype(BF16)
 
 
 def hidden_body(
-    len_ref, h_ref, gain_ref, wa_ref, wb_ref, skva_ref, skvb_ref, sq_ref, sr_ref, out_ref, last_scr
-):
-    last_scr[...] = dot(sq_ref[:, 0:512], wa_ref[:, 512:1024], LAST) + dot(
-        sq_ref[:, 512:1024], wb_ref[:, 512:1024], LAST
+    len_ref,
+    h_ref,
+    gain_ref,
+    kva_ref,
+    kvb_ref,
+    qa_ref,
+    qb_ref,
+    skva_ref,
+    skvb_ref,
+    sq_ref,
+    sr_ref,
+    out_ref,
+    last_scr,
+):
+    last_scr[...] = dot(sq_ref[:, 0:512], qa_ref[...], LAST) + dot(
+        sq_ref[:, 512:1024], qb_ref[...], LAST
     )
     pos = lax.broadcasted_iota(jnp.int32, (SEQ, 1), 0)
     for p in range(PAIRS):
         rows = slice(p * SEQ, (p + 1) * SEQ)
-        gn = dot(skva_ref[rows, :], wa_ref[:, 0:512], LAST) + dot(
-            skvb_ref[rows, :], wb_ref[:, 0:512], LAST
+        gn = dot(skva_ref[rows, :], kva_ref[...], LAST) + dot(
+            skvb_ref[rows, :], kvb_ref[...], LAST
         )
         at = pos == len_ref[p] - 1
         gn = gn + jnp.where(at, last_scr[p : p + 1, :], 0.0)
@@ -336,17 +356,20 @@
     )
 
 
-def gather_rows(x):
+def by_chip(planes):
+    got = planes.reshape(4, 4, 8, 8, -1)
+    return jnp.transpose(got, (0, 2, 1, 3, 4)).reshape(1024, -1)
+
+
+def scatter_planes(x):
     width = x.shape[1]
-    got = everyone(x, ("z", "x"), 32).reshape(256, width)
-    return everyone(got, "pb", 4).reshape(1024, width)
-
-
-def scatter_rows(x):
-    width = x.shape[1]
-    got = lax.all_to_all(x.reshape(4, 256, width), "pb", 0, 0, tiled=True)
-    part = jnp.sum(got.astype(F32), axis=0).astype(BF16)
-    got = lax.all_to_all(part.reshape(32, 8, width), ("z", "x"), 0, 0, tiled=True)
+    turned = jnp.transpose(x.reshape(4, 8, 4, 8, width), (0, 2, 1, 3, 4)).reshape(16, 64, width)
+    got = lax.all_to_all(turned, ("pb", "x"), 0, 0, tiled=True)
+    return jnp.sum(got.astype(F32), axis=0).astype(BF16)
+
+
+def scatter_z(part):
+    got = lax.all_to_all(part.reshape(8, 8, -1), "z", 0, 0, tiled=True)
     return jnp.sum(got.astype(F32), axis=0)
 
 
@@ -396,11 +419,7 @@
     block = jnp.concatenate(
         [jnp.where(first, mine, theirs), jnp.where(first, theirs, mine)], axis=0
     )
-    wa = gather_rows(block[:, 0:1024])
-    oa = gather_rows(block[:, 1024:1536])
-    wb = swap(wa)
-    ob = swap(oa)
-
+    column = everyone(block, "z", 8).reshape(64, 1536)
     normed, turned, nlast, xlast = call(
         prep_body,
         [((ROWS, D), BF16), ((D, ROWS), BF16), ((8, D), BF16), ((8, D), F32)],
@@ -408,6 +427,15 @@
         flops=10_000_000,
         nbytes=4 << 20,
     )(lens, tokens, gain)
+
+    column, normed, turned, nlast, xlast = lax.optimization_barrier(
+        (column, normed, turned, nlast, xlast)
+    )
+    kvqa = by_chip(everyone(column[:, 0:1024], ("pb", "x"), 16))
+    kva, qa = kvqa[:, 0:512], kvqa[:, 512:1024]
+    planes_o = everyone(column[:, 1024:1536], ("pb", "x"), 16)
+    kvb = swap(kva)
+    qb = swap(qa)
 
     kproj, krot, vcast, qproj, qrot, attn, ctx = pl.pallas_call(
         attend_body,
@@ -420,14 +448,18 @@
             jax.ShapeDtypeStruct((32, SEQ), F32),
             jax.ShapeDtypeStruct((8, D), BF16),
         ],
-        in_specs=[SM] + [VM] * 6,
+        in_specs=[SM] + [VM] * 8,
         out_specs=[VM] * 7,
         scratch_shapes=[pltpu.VMEM((8, D), F32), pltpu.VMEM((8, D), F32)],
-        compiler_params=pltpu.CompilerParams(vmem_limit_bytes=48 << 20),
+        compiler_params=pltpu.CompilerParams(vmem_limit_bytes=24 << 20),
         cost_estimate=pl.CostEstimate(
             flops=1_100_000_000, bytes_accessed=8 << 20, transcendentals=0
         ),
-    )(lens, normed, nlast, wa, wb, cos, sin)
+    )(lens, normed, nlast, kva, kvb, qa, qb, cos, sin)
+
+    ctx, planes_o = lax.optimization_barrier((ctx, planes_o))
+    oa = by_chip(planes_o)
+    ob = swap(oa)
 
     unit, oscale, score, tot = call(
         score_body,
@@ -450,44 +482,60 @@
         in_specs=[SM] + [VM] * 14,
         out_specs=[VM] * 4,
         scratch_shapes=[pltpu.VMEM((8, D), F32)] * 3,
-        compiler_params=pltpu.CompilerParams(vmem_limit_bytes=48 << 20),
+        compiler_params=pltpu.CompilerParams(vmem_limit_bytes=24 << 20),
         cost_estimate=pl.CostEstimate(
             flops=200_000_000, bytes_accessed=8 << 20, transcendentals=0
         ),
     )(lens, krot, vcast, kproj, qproj, qrot, attn, unit, oscale, oa, ob, fg, sv, cos, sin)
 
-    loss, grad_a, grad_b, skva, skvb, sq, sr = call(
+    half_grad = ((D, 512), BF16)
+    loss, grad_kvb, grad_qb, grad_ob, skva, skvb, sq, sr = call(
         weight_body,
         [
             ((8, HW), F32),
-            ((D, 1536), BF16),
-            ((D, 1536), BF16),
+            half_grad,
+            half_grad,
+            half_grad,
             ((ROWS, 512), BF16),
             ((ROWS, 512), BF16),
             ((8, D), BF16),
             ((8, D), F32),
         ],
         [SM] + [VM] * 10,
-        flops=1_100_000_000,
-        nbytes=12 << 20,
+        flops=600_000_000,
+        nbytes=8 << 20,
     )(pb, totals, score, teach, gkva, gkvb, gq, gr, turned, nlast, ctx)
-
-    other = swap(grad_b)
-    chip = (grad_a.astype(F32) + other.astype(F32)).astype(BF16)
-    reduced = scatter_rows(chip)
+    grad_kva, grad_qa, grad_oa = call(
+        own_weight_body,
+        [half_grad, half_grad, half_grad],
+        [VM] * 6,
+        flops=600_000_000,
+        nbytes=6 << 20,
+    )(skva, sq, sr, turned, nlast, ctx)
+
+    def chip(own, other):
+        return (own.astype(F32) + swap(other).astype(F32)).astype(BF16)
+
+    part = scatter_planes(
+        jnp.concatenate(
+            [chip(grad_kva, grad_kvb), chip(grad_qa, grad_qb), chip(grad_oa, grad_ob)], axis=1
+        )
+    )
 
     (grad_hidden,) = pl.pallas_call(
         hidden_body,
         out_shape=[jax.ShapeDtypeStruct((ROWS, D), BF16)],
-        in_specs=[SM] + [VM] * 8,
+        in_specs=[SM] + [VM] * 10,
         out_specs=[VM],
         scratch_shapes=[pltpu.VMEM((8, D), F32)],
-        compiler_params=pltpu.CompilerParams(vmem_limit_bytes=48 << 20),
+        compiler_params=pltpu.CompilerParams(vmem_limit_bytes=24 << 20),
         cost_estimate=pl.CostEstimate(
             flops=1_100_000_000, bytes_accessed=8 << 20, transcendentals=0
         ),
-    )(lens, tokens, gain, wa, wb, skva, skvb, sq, sr)
-
+    )(lens, tokens, gain, kva, kvb, qa, qb, skva, skvb, sq, sr)
+
+    part, grad_hidden = lax.optimization_barrier((part, grad_hidden))
+    reduced = scatter_z(part)
     keep = jnp.where(first, reduced[0:4], reduced[4:8])
     got = swap(jnp.where(first, reduced[4:8], reduced[0:4]))
     low = jnp.where(first, keep, got)

time: 239 us -> 206 us (0.86)
  blocking collectives: 80.1 us -> 49.6 us
  local copies, waits for them, and re-layouts: 25.1 us -> 38.1 us
  starting transfers between devices: 39.9 us -> 35.4 us
  Pallas kernels: 22.2 us -> 17.9 us
  other arithmetic: 10.2 us -> 5.98 us
  waiting for transfers between devices: 59.1 us -> 56 us
    all_to_all x1, blocking collectives: 40.7 us -> 15.9 us  [scatter_z(): got = lax.all_to_all(part.reshape(8, 8, -1), 'z', 0, 0, tiled=True)]
    all_to_all x3, waiting for transfers between devices: 33.6 us -> 11.5 us  [everyone(): lax.all_to_all(jnp.broadcast_to(x[None], (count, *x.shape)), axes, 0, 0,...]
    all_to_all x1, waiting for transfers between devices: 19.1 us -> 38.4 us  [scatter_planes(): got = lax.all_to_all(turned, ('pb', 'x'), 0, 0, tiled=True)]
    unnamed x72 -> x88, local copies, waits for them, and re-layouts: 19.2 us -> 28 us
    all_to_all x2 -> x1, blocking collectives: 39.5 us -> 33.8 us  [everyone(): lax.all_to_all(jnp.broadcast_to(x[None], (count, *x.shape)), axes, 0, 0,...]
    all_to_all x1, starting transfers between devices: 8.73 us -> 5.1 us  [scatter_planes(): got = lax.all_to_all(turned, ('pb', 'x'), 0, 0, tiled=True)]
    reduce_sum x2, other arithmetic: 4.78 us -> 2.37 us  [the longest x1 2.34 us: scatter_planes(): return jnp.sum(got.astype(F32), axis=0).astype(BF16)]
    pallas_call x1 -> x2, Pallas kernels: 5.09 us -> 2.76 us  [the longest x1 1.51 us: shards(): call(weight_body, [((8, HW), F32), half_grad, half_grad, half_grad, ((ROW...]
  transfers between devices with their start and end apart: 9 -> 12, of which waited for: 6 -> 9; matrix products, arithmetic and copies ran while one was open for 1% -> 2% of each run, Pallas kernels for 7% -> 8%
where the time goes in v2:
time: 206 us; the launch traced here: 204 us
  waiting for transfers between devices  56 us (27%)
  blocking collectives  49.6 us (24%)
  local copies, waits for them, and re-layouts  38.1 us (18%)
  starting transfers between devices  35.4 us (17%)
  Pallas kernels  17.9 us (9%)
  other arithmetic  5.98 us (3%)
    all_to_all x1, waiting for transfers between devices, scatter_planes(): got = lax.all_to_all(turned, ('pb', 'x'), 0, 0, tiled=True)  38.4 us
    all_to_all x1, blocking collectives, everyone(): lax.all_to_all(jnp.broadcast_to(x[None], (count, *x.shape)), axes, 0, 0,...  33.8 us
    unnamed x88, local copies, waits for them, and re-layouts  28 us
    all_to_all x3, starting transfers between devices, everyone(): lax.all_to_all(jnp.broadcast_to(x[None], (count, *x.shape)), axes, 0, 0,...  16.1 us
    all_to_all x1, blocking collectives, scatter_z(): got = lax.all_to_all(part.reshape(8, 8, -1), 'z', 0, 0, tiled=True)  15.9 us
    ppermute x8, starting transfers between devices, swap(): return lax.ppermute(x, 'c', [(0, 1), (1, 0)])  14.2 us
    all_to_all x3, waiting for transfers between devices, everyone(): lax.all_to_all(jnp.broadcast_to(x[None], (count, *x.shape)), axes, 0, 0,...  11.5 us
    ppermute x8, waiting for transfers between devices, swap(): return lax.ppermute(x, 'c', [(0, 1), (1, 0)])  6.05 us
  transfers between devices with their start and end apart: 12, of which 9 were waited for; matrix products, arithmetic and copies ran while one was open for 2% of the time, Pallas kernels for 8%

profile of v2, /device:TPU:1, one launch (start us, length us, event | category | flops | bytes accessed | tf_op | source)
XLA Modules:
  0.0 204.1 jit_solution(4179713693831168992)
XLA Ops:
  2.1 3.3 %collective-permute-start = (bf16[4,1536]{1,0:T(4,128)(2,1)S(1)}, bf16[4,1536]{1,0:T(4,128)(2,1)S(1)}, u32[]{:S(2)}, u32[]{:S(2)}) collective-permute-start(bf16[4,1536]{1,0:T(4,128)(2,1)S(1)} %broadcast_select_fusion.4), channel_id=1, source_target_pairs={{0,1},{1,0},{2,3},{3,2},{4,5},{5,4},{6,7},{7,6},{8,9},{9,8},{10,11... | collective-permute-start | bytes 36872 | tf_op jit(solution)/shard_map/ppermute | solution.py:377
  7.0 6.5 %all-to-all-start = ((bf16[8,8,1536]{2,1,0:T(8,128)(2,1)}), bf16[8,8,1536]{2,1,0:T(8,128)(2,1)S(1)}, u32[]{:S(2)}, u32[]{:S(2)}) async-start(bf16[8,8,1536]{2,1,0:T(8,128)(2,1)} %broadcast_in_dim.21), calls=%async_computation | async-start | bytes 393216 | tf_op jit(solution)/shard_map/all_to_all | solution.py:354
  16.1 1.3 shard_map.171
  19.3 3.6 %all-to-all-done = bf16[8,8,1536]{2,1,0:T(8,128)(2,1)S(1)} async-done(((bf16[8,8,1536]{2,1,0:T(8,128)(2,1)}), bf16[8,8,1536]{2,1,0:T(8,128)(2,1)S(1)}, u32[]{:S(2)}, u32[]{:S(2)}) %all-to-all-start) | async-done | bytes 196640 | tf_op jit(solution)/shard_map/all_to_all | solution.py:354
  23.2 33.8 %all_to_all.30 = bf16[16,64,1024]{2,1,0:T(8,128)(2,1)S(1)} all-to-all(bf16[16,64,1024]{2,1,0:T(8,128)(2,1)S(1)} %broadcast_in_dim.23), channel_id=1, replica_groups=mesh['pb'=4,'z'=8,'x'=4,'c'=2] {'pb','x'}, dimensions={0} | all-to-all | bytes 4194304 | tf_op jit(solution)/shard_map/all_to_all | solution.py:354
  57.5 3.2 %collective-permute-start.1 = (bf16[1024,512]{1,0:T(8,128)(2,1)S(1)}, bf16[1024,512]{1,0:T(8,128)(2,1)S(1)}, u32[]{:S(2)}, u32[]{:S(2)}) collective-permute-start(bf16[1024,512]{1,0:T(8,128)(2,1)S(1)} %get-tuple-element.86.kva_ref), channel_id=1, source_target_pairs={{0,1},{1,0},{2,3},{3,2},{4,5},{5,4},{6,7},{7,6},{8,9},{9,8},{10,11... | collective-permute-start | bytes 3145736 | tf_op jit(solution)/shard_map/ppermute | solution.py:377
  62.7 4.3 %all-to-all-start.2 = ((bf16[16,64,512]{2,1,0:T(8,128)(2,1)}), bf16[16,64,512]{2,1,0:T(8,128)(2,1)}, u32[]{:S(2)}, u32[]{:S(2)}) async-start(bf16[16,64,512]{2,1,0:T(8,128)(2,1)} %broadcast_in_dim.48), calls=%async_computation.2 | async-start | bytes 2097152 | tf_op jit(solution)/shard_map/all_to_all | solution.py:354
  67.2 1.6 copy-done.15
  68.7 4.4 %shard_map.172 = (f32[512,512]{1,0:T(8,128)S(1)}, bf16[512,512]{1,0:T(8,128)(2,1)S(1)}, bf16[512,512]{1,0:T(8,128)(2,1)S(1)}, f32[8,1024]{1,0:T(8,128)S(1)}, bf1...) custom-call(s32[4]{0:T(128)S(1)} %bitcast.43, bf16[512,1024]{1,0:T(8,128)(2,1)S(1)} %copy-done.15, ...), custom_call_target="tpu_custom_call" | custom-call | flops 1100000000 | bytes 8388608 | tf_op jit(solution)/shard_map/pallas_call | solution.py:440
  76.3 7.7 %all-to-all-done.2 = bf16[16,64,512]{2,1,0:T(8,128)(2,1)} async-done(((bf16[16,64,512]{2,1,0:T(8,128)(2,1)}), bf16[16,64,512]{2,1,0:T(8,128)(2,1)}, u32[]{:S(2)}, u32[]{:S(2)}) %all-to-all-start.2) | async-done | bytes 1048608 | tf_op jit(solution)/shard_map/all_to_all | solution.py:354
  83.9 1.4 copy.26
  85.3 1.9 collective-permute-start.3
  87.2 2.3 %collective-permute-done.3.ob_ref = bf16[1024,512]{1,0:T(8,128)(2,1)S(1)} collective-permute-done((bf16[1024,512]{1,0:T(8,128)(2,1)S(1)}, bf16[1024,512]{1,0:T(8,128)(2,1)S(1)}, u32[]{:S(2)}, u32[]{:S(2)}) %collective-permute-start.3) | collective-permute-done | bytes 1048608 | tf_op jit(solution)/shard_map/ppermute | solution.py:377
  92.2 5.3 %all-to-all-start.3 = ((f32[256,1,128]{2,1,0:T(1,128)}), f32[256,1,128]{2,1,0:T(1,128)S(1)}, u32[]{:S(2)}, u32[]{:S(2)}) async-start(f32[256,1,128]{2,1,0:T(1,128)} %broadcast_in_dim.53), calls=%async_computation.3 | async-start | bytes 262144 | tf_op jit(solution)/shard_map/all_to_all | solution.py:354
  104.8 2.8 %shard_map.174 = (f32[512,512]{1,0:T(8,128)S(1)}, f32[512,512]{1,0:T(8,128)S(1)}, f32[8,1024]{1,0:T(8,128)S(1)}, f32[8,1024]{1,0:T(8,128)S(1)}) custom-call(s32[4]{0:T(128)S(1)} %bitcast.44, bf16[512,512]{1,0:T(8,128)(2,1)S(1)} %copy-done.21, bf16[512,512]{1,0:T(8,128)(2,1)S(1)} %copy-done.23, f32[512,512]{1,0:T(8,128)S(1)} %copy-done.13, ...), custom_call_target="tpu_custom_call" | custom-call | flops 200000000 | bytes 8388608 | tf_op jit(solution)/shard_map/pallas_call | solution.py:474
  114.9 1.5 shard_map.175
  116.4 2.1 %collective-permute-start.4 = (bf16[1024,512]{1,0:T(8,128)(2,1)S(1)}, bf16[1024,512]{1,0:T(8,128)(2,1)S(1)}, u32[]{:S(2)}, u32[]{:S(2)}) collective-permute-start(bf16[1024,512]{1,0:T(8,128)(2,1)S(1)} %get-tuple-element.77), channel_id=1, source_target_pairs={{0,1},{1,0},{2,3},{3,2},{4,5},{5,4},{6,7},{7,6},{8,9},{9,8},{10,11... | collective-permute-start | bytes 3145736 | tf_op jit(solution)/shard_map/ppermute | solution.py:377
  124.4 2.1 %copy.27 = bf16[4,8,4,8,1536]{4,3,1,2,0:T(8,128)(2,1)} copy(bf16[4,8,4,8,1536]{4,3,2,1,0:T(8,128)(2,1)S(1)} %bitcast.47) | data formatting | bytes 6291456 | tf_op jit(solution)/shard_map/reshape | solution.py:366
  126.5 5.1 %all-to-all-start.4 = ((bf16[16,64,1536]{2,1,0:T(8,128)(2,1)}), bf16[16,64,1536]{2,1,0:T(8,128)(2,1)}, u32[]{:S(2)}, u32[]{:S(2)}) async-start(bf16[16,64,1536]{2,1,0:T(8,128)(2,1)} %bitcast.46), calls=%async_computation.4 | async-start | bytes 6291456 | tf_op jit(solution)/shard_map/all_to_all | solution.py:367
  134.9 5.9 %shard_map.177 = bf16[512,1024]{1,0:T(8,128)(2,1)} custom-call(s32[4]{0:T(128)S(1)} %bitcast.45, bf16[512,1024]{1,0:T(8,128)(2,1)S(1)} %bitcast.34, f32[1,1024]{1,0:T(1,128)S(1)} %bitcast.37, bf16[1024,512]{1,0:T(8,128)(2,1)S(1)} %get-tuple-element.86.kva_ref, bf16[1024,512]{1,0:T(8,128)(2,1)S(1)} %copy-done.3, ...), custom_call_target="tpu_custom_call" | custom-call | flops 1100000000 | bytes 8388608 | tf_op jit(solution)/shard_map/pallas_call | solution.py:525
  140.8 38.4 %all-to-all-done.4 = bf16[16,64,1536]{2,1,0:T(8,128)(2,1)} async-done(((bf16[16,64,1536]{2,1,0:T(8,128)(2,1)}), bf16[16,64,1536]{2,1,0:T(8,128)(2,1)}, u32[]{:S(2)}, u32[]{:S(2)}) %all-to-all-start.4) | async-done | bytes 3145760 | tf_op jit(solution)/shard_map/all_to_all | solution.py:367
  179.3 2.3 %reduce_sum.21 = bf16[64,1536]{1,0:T(8,128)(2,1)S(1)} reduce(bf16[16,64,1536]{2,1,0:T(8,128)(2,1)} %all-to-all-done.4, bf16[]{:T(256)} %constant.20.clone.1), dimensions={0}, to_apply=%region_0.1 | reduce | flops 1474560 | bytes 3342338 | tf_op jit(solution)/shard_map/reduce_sum | solution.py:368
  181.6 15.9 %all_to_all.31 = bf16[8,8,1536]{2,1,0:T(8,128)(2,1)S(1)} all-to-all(bf16[8,8,1536]{2,1,0:T(8,128)(2,1)S(1)} %bitcast.51), channel_id=1, replica_groups=mesh['pb'=4,'z'=8,'x'=4,'c'=2] {'z'}, dimensions={0} | all-to-all | bytes 393216 | tf_op jit(solution)/shard_map/all_to_all | solution.py:372
  197.5 3.0 %collective-permute-start.7 = (f32[4,1536]{1,0:T(4,128)S(1)}, f32[4,1536]{1,0:T(4,128)S(1)}, u32[]{:S(2)}, u32[]{:S(2)}) collective-permute-start(f32[4,1536]{1,0:T(4,128)S(1)} %slice_select_fusion), channel_id=1, source_target_pairs={{0,1},{1,0},{2,3},{3,2},{4,5},{5,4},{6,7},{7,6},{8,9},{9,8},{10,11... | collective-permute-start | bytes 73736 | tf_op jit(solution)/shard_map/ppermute | solution.py:377
  (133 shorter events, 43.5 us)
Async XLA Ops:
  2.1 4.2 %collective-permute-start = (bf16[4,1536]{1,0:T(4,128)(2,1)S(1)}, bf16[4,1536]{1,0:T(4,128)(2,1)S(1)}, u32[]{:S(2)}, u32[]{:S(2)}) collective-permute-start(bf16[4,1536]{1,0:T(4,128)(2,1)S(1)} %broadcast_select_fusion.4), channel_id=1, source_target_pairs={{0,1},{1,0},{2,3},{3,2},{4,5},{5,4},{6,7},{7,6},{8,9},{9,8},{10,11... | collective-permute-start | bytes 36872 | tf_op jit(solution)/shard_map/ppermute | solution.py:377
  7.0 15.9 %all-to-all-start = ((bf16[8,8,1536]{2,1,0:T(8,128)(2,1)}), bf16[8,8,1536]{2,1,0:T(8,128)(2,1)S(1)}, u32[]{:S(2)}, u32[]{:S(2)}) async-start(bf16[8,8,1536]{2,1,0:T(8,128)(2,1)} %broadcast_in_dim.21), calls=%async_computation | async-start | bytes 393216 | tf_op jit(solution)/shard_map/all_to_all | solution.py:354
  23.0 34.0 %copy-start.42 = (bf16[8,8,1536]{2,1,0:T(8,128)(2,1)}, bf16[8,8,1536]{2,1,0:T(8,128)(2,1)S(1)}, u32[]{:S(2)}) copy-start(bf16[8,8,1536]{2,1,0:T(8,128)(2,1)S(1)} %all-to-all-done) | copy-start | bytes 589828
  57.4 9.7 %copy-start.24 = (f32[128,128]{1,0:T(8,128)S(1)}, f32[128,128]{1,0:T(8,128)}, u32[]{:S(2)}) copy-start(f32[128,128]{1,0:T(8,128)} %constant.21.clone.cos_ref) | copy-start | bytes 196612
  57.4 9.7 %copy-start.25 = (f32[128,128]{1,0:T(8,128)S(1)}, f32[128,128]{1,0:T(8,128)}, u32[]{:S(2)}) copy-start(f32[128,128]{1,0:T(8,128)} %constant.22.clone.sin_ref) | copy-start | bytes 196612
  57.5 9.7 %copy-start.37 = (s32[1,4]{1,0:T(1,128)S(1)}, s32[1,4]{1,0:T(1,128)}, u32[]{:S(2)}) copy-start(s32[1,4]{1,0:T(1,128)} %param.13) | copy-start | bytes 52
  57.5 9.6 %collective-permute-start.1 = (bf16[1024,512]{1,0:T(8,128)(2,1)S(1)}, bf16[1024,512]{1,0:T(8,128)(2,1)S(1)}, u32[]{:S(2)}, u32[]{:S(2)}) collective-permute-start(bf16[1024,512]{1,0:T(8,128)(2,1)S(1)} %get-tuple-element.86.kva_ref), channel_id=1, source_target_pairs={{0,1},{1,0},{2,3},{3,2},{4,5},{5,4},{6,7},{7,6},{8,9},{9,8},{10,11... | collective-permute-start | bytes 3145736 | tf_op jit(solution)/shard_map/ppermute | solution.py:377
  60.7 6.4 %collective-permute-start.2 = (bf16[1024,512]{1,0:T(8,128)(2,1)S(1)}, bf16[1024,512]{1,0:T(8,128)(2,1)}, u32[]{:S(2)}, u32[]{:S(2)}) collective-permute-start(bf16[1024,512]{1,0:T(8,128)(2,1)S(1)} %get-tuple-element.85.qa_ref), channel_id=1, source_target_pairs={{0,1},{1,0},{2,3},{3,2},{4,5},{5,4},{6,7},{7,6},{8,9},{9,8},{10,11... | collective-permute-start | bytes 3145736 | tf_op jit(solution)/shard_map/ppermute | solution.py:377
  62.7 21.2 %all-to-all-start.2 = ((bf16[16,64,512]{2,1,0:T(8,128)(2,1)}), bf16[16,64,512]{2,1,0:T(8,128)(2,1)}, u32[]{:S(2)}, u32[]{:S(2)}) async-start(bf16[16,64,512]{2,1,0:T(8,128)(2,1)} %broadcast_in_dim.48), calls=%async_computation.2 | async-start | bytes 2097152 | tf_op jit(solution)/shard_map/all_to_all | solution.py:354
  67.1 6.0 %copy-start.2 = (bf16[1024,512]{1,0:T(8,128)(2,1)}, bf16[1024,512]{1,0:T(8,128)(2,1)S(1)}, u32[]{:S(2)}) copy-start(bf16[1024,512]{1,0:T(8,128)(2,1)S(1)} %collective-permute-done.1.kvb_ref) | copy-start | bytes 3145732
  76.3 14.2 %copy-start.32 = (f32[32,128]{1,0:T(8,128)}, f32[32,128]{1,0:T(8,128)S(1)}, u32[]{:S(2)}) copy-start(f32[32,128]{1,0:T(8,128)S(1)} %get-tuple-element.64.attn_ref) | copy-start | bytes 49156
  76.3 11.0 %copy-start.43 = (f32[1,4]{1,0:T(1,128)S(1)}, f32[1,4]{1,0:T(1,128)}, u32[]{:S(2)}) copy-start(f32[1,4]{1,0:T(1,128)} %param.14) | copy-start | bytes 52
  76.3 13.3 %copy-start.34 = (f32[1024]{0:T(1024)S(1)}, f32[1024]{0:T(1024)}, u32[]{:S(2)}) copy-start(f32[1024]{0:T(1024)} %param.16) | copy-start | bytes 12292
  76.3 13.3 %copy-start.35 = (f32[1024]{0:T(1024)S(1)}, f32[1024]{0:T(1024)}, u32[]{:S(2)}) copy-start(f32[1024]{0:T(1024)} %param.17) | copy-start | bytes 12292
  85.3 4.2 %collective-permute-start.3 = (bf16[1024,512]{1,0:T(8,128)(2,1)S(1)}, bf16[1024,512]{1,0:T(8,128)(2,1)S(1)}, u32[]{:S(2)}, u32[]{:S(2)}) collective-permute-start(bf16[1024,512]{1,0:T(8,128)(2,1)S(1)} %bitcast.30), channel_id=1, source_target_pairs={{0,1},{1,0},{2,3},{3,2},{4,5},{5,4},{6,7},{7,6},{8,9},{9,8},{10,11... | collective-permute-start | bytes 3145736 | tf_op jit(solution)/shard_map/ppermute | solution.py:377
  91.5 6.1 %copy-start.40 = (f32[8,128]{1,0:T(8,128)}, f32[8,128]{1,0:T(8,128)S(1)}, u32[]{:S(2)}) copy-start(f32[8,128]{1,0:T(8,128)S(1)} %get-tuple-element.66.oscale_ref) | copy-start | bytes 12292
  92.2 18.3 %all-to-all-start.3 = ((f32[256,1,128]{2,1,0:T(1,128)}), f32[256,1,128]{2,1,0:T(1,128)S(1)}, u32[]{:S(2)}, u32[]{:S(2)}) async-start(f32[256,1,128]{2,1,0:T(1,128)} %broadcast_in_dim.53), calls=%async_computation.3 | async-start | bytes 262144 | tf_op jit(solution)/shard_map/all_to_all | solution.py:354
  116.4 4.4 %collective-permute-start.4 = (bf16[1024,512]{1,0:T(8,128)(2,1)S(1)}, bf16[1024,512]{1,0:T(8,128)(2,1)S(1)}, u32[]{:S(2)}, u32[]{:S(2)}) collective-permute-start(bf16[1024,512]{1,0:T(8,128)(2,1)S(1)} %get-tuple-element.77), channel_id=1, source_target_pairs={{0,1},{1,0},{2,3},{3,2},{4,5},{5,4},{6,7},{7,6},{8,9},{9,8},{10,11... | collective-permute-start | bytes 3145736 | tf_op jit(solution)/shard_map/ppermute | solution.py:377
  118.6 3.8 %collective-permute-start.5 = (bf16[1024,512]{1,0:T(8,128)(2,1)S(1)}, bf16[1024,512]{1,0:T(8,128)(2,1)S(1)}, u32[]{:S(2)}, u32[]{:S(2)}) collective-permute-start(bf16[1024,512]{1,0:T(8,128)(2,1)S(1)} %get-tuple-element.79), channel_id=1, source_target_pairs={{0,1},{1,0},{2,3},{3,2},{4,5},{5,4},{6,7},{7,6},{8,9},{9,8},{10,11... | collective-permute-start | bytes 3145736 | tf_op jit(solution)/shard_map/ppermute | solution.py:377
  118.8 5.0 %collective-permute-start.6 = (bf16[1024,512]{1,0:T(8,128)(2,1)S(1)}, bf16[1024,512]{1,0:T(8,128)(2,1)S(1)}, u32[]{:S(2)}, u32[]{:S(2)}) collective-permute-start(bf16[1024,512]{1,0:T(8,128)(2,1)S(1)} %get-tuple-element.81), channel_id=1, source_target_pairs={{0,1},{1,0},{2,3},{3,2},{4,5},{5,4},{6,7},{7,6},{8,9},{9,8},{10,11... | collective-permute-start | bytes 3145736 | tf_op jit(solution)/shard_map/ppermute | solution.py:377
  126.5 5.1 %copy-start.29 = (f32[1024]{0:T(1024)S(1)}, f32[1024]{0:T(1024)}, u32[]{:S(2)}) copy-start(f32[1024]{0:T(1024)} %param.15) | copy-start | bytes 12292
  126.5 5.1 %copy-start.39 = (s32[1,4]{1,0:T(1,128)S(1)}, s32[1,4]{1,0:T(1,128)}, u32[]{:S(2)}) copy-start(s32[1,4]{1,0:T(1,128)} %param.13) | copy-start | bytes 52
  126.5 52.8 %all-to-all-start.4 = ((bf16[16,64,1536]{2,1,0:T(8,128)(2,1)}), bf16[16,64,1536]{2,1,0:T(8,128)(2,1)}, u32[]{:S(2)}, u32[]{:S(2)}) async-start(bf16[16,64,1536]{2,1,0:T(8,128)(2,1)} %bitcast.46), calls=%async_computation.4 | async-start | bytes 6291456 | tf_op jit(solution)/shard_map/all_to_all | solution.py:367
  197.5 4.1 %collective-permute-start.7 = (f32[4,1536]{1,0:T(4,128)S(1)}, f32[4,1536]{1,0:T(4,128)S(1)}, u32[]{:S(2)}, u32[]{:S(2)}) collective-permute-start(f32[4,1536]{1,0:T(4,128)S(1)} %slice_select_fusion), channel_id=1, source_target_pairs={{0,1},{1,0},{2,3},{3,2},{4,5},{5,4},{6,7},{7,6},{8,9},{9,8},{10,11... | collective-permute-start | bytes 73736 | tf_op jit(solution)/shard_map/ppermute | solution.py:377
  (32 other events, 42.5 us)
